TPU v7x, 32 devices: a whole 2x2x4 slice. The times are simulated.
32 devices in a mesh: seq: 8 (over y, x, core), exp: 4 (over z).
Axes of the slice: x: 2, y: 2, z: 4, core: 2. Of those that a mesh axis runs over, the one named last changes fastest.
Arguments:
- layer_input: bfloat16 [4, 4096, 768], P('exp', 'seq'), may hold values from -6 to 6
- token_ids: int32 [4, 4096], P('exp', 'seq'), may hold values from 0 to 8007, as said below
- segment_ids: int32 [4, 4096], P('exp'), may hold values from 0 to 7, never falling along the last dimension, each value on 1 to 1024 neighbouring positions
- hash_table: int32 [8008], replicated, may hold values from 0 to 3, as said below
- first_gain: float32 [768], replicated, may hold values from 0.25 to 1.75
- first_bias: float32 [768], replicated, may hold values from -1.5 to 1.5
- second_gain: float32 [768], replicated, may hold values from 0.25 to 1.75
- second_bias: float32 [768], replicated, may hold values from -1.5 to 1.5
- w_qkv: bfloat16 [768, 2304], replicated, may hold values from -0.21875 to 0.21875
- w_out: bfloat16 [768, 768], replicated, may hold values from -3 to 3
- w_up: bfloat16 [4, 768, 3072], P('exp'), may hold values from -0.21875 to 0.21875
- w_down: bfloat16 [4, 3072, 768], P('exp'), may hold values from -0.109375 to 0.109375
- cotangent: bfloat16 [4, 4096, 768], P('exp', 'seq'), may hold values from -6 to 6
Outputs:
- layer_output: bfloat16 [4, 4096, 768], P('exp', 'seq')
- grad_input: float32 [4, 4096, 768], P('exp', 'seq')
- grad_w_qkv: float32 [768, 2304], replicated
- grad_w_out: float32 [768, 768], replicated
- grad_first_gain: float32 [768], replicated
- grad_first_bias: float32 [768], replicated
- grad_second_gain: float32 [768], replicated
- grad_second_bias: float32 [768], replicated
- grad_w_up: float32 [4, 768, 3072], P('exp')
- grad_w_down: float32 [4, 3072, 768], P('exp')
Inputs may be any that keep to these rules, and one draw needn't show every extreme that they name: `token_ids`: token ids range over the vocabulary. Among the 512 positions that one device holds, hash_table sends exactly 256 to one expert, the same expert on all devices that hold the same positions of their sequences, and the other experts' counts differ from one another by at most one. `hash_table`: every expert is named by 2002 token ids. `segment_ids`: numbers never fall along a sequence; each document holds 1 to 1024 neighbouring positions, and one in every sequence holds exactly 1024.
All inputs are finite; a program needn't handle non-finite values.
Results may differ from a plain program's by a relative error of at most 0.017.
Values may be sent and summed in bfloat16 or wider, within the bound.
No kernel may reach another device: no remote copies, remote signals or barrier semaphores. Data moves between devices by JAX's collectives and lax.ppermute only.
A program may use at most 192 MiB of HBM per device.

v0:
```python
import functools
import math

import jax
import jax.numpy as jnp
from jax import lax
from jax.experimental import pallas as pl
from jax.experimental.pallas import tpu as pltpu
from jax.sharding import PartitionSpec as P

HEADS = 12
HEAD_DIM = 64
DOC_MOST = 1024
EPSILON = 1e-05
LOW = -1e30
LOWER = -2e30
LANES = 128
TILE = 256
F32 = jnp.float32
BF16 = jnp.bfloat16
MIB = 1 << 20
COST = 1


def dot(a, b):
    return lax.dot_general(a, b, (((1,), (0,)), ((), ())), preferred_element_type=F32)


def dot_nt(a, b):
    return lax.dot_general(a, b, (((1,), (1,)), ((), ())), preferred_element_type=F32)


def dot_tn(a, b):
    return lax.dot_general(a, b, (((0,), (0,)), ((), ())), preferred_element_type=F32)


def iota(shape, axis):
    return lax.broadcasted_iota(jnp.int32, shape, axis)


def one_hot(ids, width):
    return jnp.where(iota((ids.shape[0], width), 1) == ids, 1.0, 0.0).astype(BF16)


def norm_rows(values):
    center = values - jnp.mean(values, axis=-1, keepdims=True)
    scale = lax.rsqrt(jnp.mean(center * center, axis=-1, keepdims=True) + EPSILON)
    return center * scale, scale


def norm_back(grad, normed, scale):
    inner = jnp.mean(grad * normed, axis=-1, keepdims=True)
    return scale * (grad - jnp.mean(grad, axis=-1, keepdims=True) - normed * inner)


def after(value, *others):
    return lax.optimization_barrier((value, others))[0]


def shape(dims, dtype):
    return jax.ShapeDtypeStruct(dims, dtype)


def call(body, name, out_shape, args, *, grid=(), in_specs=None, out_specs=None, scratch=(),
         scalars=0, aliases=None, flops=0, nbytes=0, special=0, vmem=56):
    outs = out_shape if isinstance(out_shape, (tuple, list)) else [out_shape]
    whole = pl.BlockSpec(memory_space=pltpu.VMEM)
    if in_specs is None:
        in_specs = [whole] * (len(args) - scalars)
    if out_specs is None:
        out_specs = [whole] * len(outs)
        if not isinstance(out_shape, (tuple, list)):
            out_specs = out_specs[0]
    return pl.pallas_call(
        body,
        name=name,
        out_shape=out_shape,
        grid_spec=pltpu.PrefetchScalarGridSpec(
            num_scalar_prefetch=scalars,
            grid=grid,
            in_specs=in_specs,
            out_specs=out_specs,
            scratch_shapes=scratch,
        ),
        input_output_aliases=aliases or {},
        cost_estimate=pl.CostEstimate(flops=COST, bytes_accessed=COST, transcendentals=0),
        compiler_params=pltpu.CompilerParams(vmem_limit_bytes=vmem * MIB),
    )(*args)


def column(row):
    return jnp.broadcast_to(row.astype(F32), (8, row.shape[1])).T[:, :1].astype(jnp.int32)


def route_body(parts, capacity, docs, at_ref, ids_ref, table_ref, rows_ref, segment_ref, slot_ref,
               low_ref, tall_ref, meta_ref, *out_refs):
    ids = column(ids_ref[...])
    count = ids.shape[0]
    lines = table_ref.shape[0]
    picked = dot(one_hot(ids >> 7, lines), table_ref[...].astype(F32).astype(BF16))
    lane = iota((count, LANES), 1)
    choice = jnp.sum(
        jnp.where(lane == (ids & (LANES - 1)), picked, 0.0), axis=1, keepdims=True
    ).astype(jnp.int32)
    mine = lane == choice
    below = jnp.where(iota((count, count), 0) > iota((count, count), 1), 1.0, 0.0).astype(BF16)
    ranks = dot(below, jnp.where(mine, 1.0, 0.0).astype(BF16))
    rank = jnp.sum(jnp.where(mine, ranks, 0.0), axis=1, keepdims=True).astype(jnp.int32)
    slot = (choice ^ at_ref[0]) * capacity + rank
    slot_ref[...] = slot
    rows = rows_ref[...]
    for k in range(parts):
        chosen = one_hot(slot - k * capacity, capacity)
        out_refs[k][...] = dot_tn(chosen, rows).astype(BF16)

    pair_len = low_ref.shape[1]
    pair_at = pl.multiple_of(at_ref[2] * pair_len, pair_len)
    segments = segment_ref[...]
    here = segment_ref[:, pl.ds(pair_at, pair_len)]
    low = jnp.zeros((1, pair_len), F32)
    for d in range(docs):
        start = jnp.sum(jnp.where(segments < d, 1.0, 0.0), axis=1, keepdims=True)
        low = low + jnp.where(here == d, start, 0.0)
    low = low.astype(jnp.int32) - (pair_at - pair_len)
    low_ref[...] = low
    tall_ref[...] = column(low)
    place = iota((1, LANES), 1)
    meta = jnp.where(place == 0, at_ref[1], 0)
    for t in range(pair_len // TILE):
        meta = jnp.where(place == 1 + t, low[:, t * TILE : t * TILE + 1] >> 8, meta)
    meta_ref[...] = meta


def route(at, ids, table, rows, segments, parts, capacity, docs):
    count, width = rows.shape
    pair_len = 2 * count
    outs = [shape((count, 1), jnp.int32), shape((1, pair_len), jnp.int32),
            shape((pair_len, 1), jnp.int32), shape((1, LANES), jnp.int32)]
    outs += [shape((capacity, width), BF16)] * parts
    return call(
        functools.partial(route_body, parts, capacity, docs), "route", outs,
        (at, ids, table, rows, segments), scalars=1,
    )


def vector(ref, at):
    lines = ref.shape[0] // 4
    return jnp.concatenate([ref[at * lines + j : at * lines + j + 1, :] for j in range(lines)], axis=1)


def project_body(skip, core_ref, own_ref, sib_ref, norm_ref, wq_ref, wk_ref, wv_ref, *refs):
    outs = refs[skip:-1]
    held_ref = refs[-1]
    step = pl.program_id(0)
    half = (pl.num_programs(0) - 1) // 2
    before = held_ref[(step + 1) % 2]
    outs[1][...] = dot(before, wk_ref[...]).astype(BF16)
    outs[2][...] = dot(before, wv_ref[...]).astype(BF16)
    if not skip:
        outs[3][...] = dot(before, wq_ref[...]).astype(BF16)
    rows = jnp.where(step < half, own_ref[...], sib_ref[...])
    normed, unused = norm_rows(rows.astype(F32))
    a = (normed * vector(norm_ref, 0) + vector(norm_ref, 1)).astype(BF16)
    held_ref[step % 2] = a
    outs[0][...] = a


def project(core, own, sib, norms, w_qkv, made):
    count, width = own.shape
    mine = width // 2
    half = count // TILE
    base = 0 if made else 2 * half

    def place(i, c):
        return ((i // half) ^ c[0]) * half + i % half

    def now(i, c):
        return (base + place(jnp.minimum(i, 2 * half - 1), c), 0)

    def then(i, c):
        return (base + place(jnp.maximum(i - 1, 0), c), 0)

    in_specs = [
        pl.BlockSpec((TILE, width), lambda i, c: (jnp.minimum(i, half - 1), 0)),
        pl.BlockSpec((TILE, width), lambda i, c: (jnp.clip(i - half, 0, half - 1), 0)),
        pl.BlockSpec(norms.shape, lambda i, c: (0, 0)),
    ] + [
        pl.BlockSpec((width, mine), functools.partial(lambda t, i, c: (0, 2 * t + c[0]), t))
        for t in range(3)
    ]
    args = [core, own, sib, norms, w_qkv, w_qkv, w_qkv]
    outs = [shape((4 * count, width), BF16)] + [shape((4 * count, mine), BF16)] * 2
    out_specs = [
        pl.BlockSpec((TILE, width), now),
        pl.BlockSpec((TILE, mine), then),
        pl.BlockSpec((TILE, mine), then),
    ]
    aliases = {}
    if made:
        in_specs += [pl.BlockSpec(memory_space=pl.ANY)] * 3
        aliases = {7: 0, 8: 1, 9: 2}
        args += list(made)
    else:
        outs.append(shape((2 * count, mine), BF16))
        out_specs.append(
            pl.BlockSpec((TILE, mine), lambda i, c: (place(jnp.maximum(i - 1, 0), c), 0))
        )
    return call(
        functools.partial(project_body, 3 if made else 0), "project", outs, args,
        grid=(2 * half + 1,), in_specs=in_specs, out_specs=out_specs, scalars=1, aliases=aliases,
        scratch=[pltpu.VMEM((2, TILE, width), BF16)],
    )


def masked_heads(block):
    lane = iota(block.shape, 1)
    zero = jnp.zeros((), block.dtype)
    return [
        jnp.where(lane < HEAD_DIM, block, zero),
        jnp.where(lane < HEAD_DIM, zero, block),
    ]


def flip(block):
    return block.astype(F32).T.astype(block.dtype)


def lanes_of(group):
    return slice(group * LANES, (group + 1) * LANES)


def put_heads(heads_ref, q_ref):
    def some(t, unused):
        here = pl.ds(pl.multiple_of(t * TILE, TILE), TILE)
        block = q_ref[here, :] * jnp.asarray(HEAD_DIM**-0.5, BF16)
        for g in range(q_ref.shape[1] // LANES):
            for h, part in enumerate(masked_heads(block[:, lanes_of(g)])):
                heads_ref[2 * g + h, here, :] = part
        return unused

    lax.fori_loop(0, q_ref.shape[0] // TILE, some, 0)


def tile_mask(begin, low, high):
    place = begin + iota((TILE, TILE), 0)
    return (place >= low) & (place <= high)


def attend_body(meta_ref, q_ref, k_ref, v_ref, lo_ref, own_ref, sib_ref, all_ref, tall_ref,
                log_ref, heads_ref, acc_ref, rows_ref):
    total, mine = q_ref.shape
    half = total // 2
    heads = range(mine // HEAD_DIM)
    put_heads(heads_ref, q_ref)
    core = meta_ref[0, 0]

    def tile(t, unused):
        at = pl.multiple_of(t * TILE, TILE)
        here = pl.ds(at, TILE)
        low = lo_ref[here, :]
        high = total + at + iota((TILE, 1), 0)
        acc_ref[...] = jnp.zeros_like(acc_ref)

        def step(j, state):
            begin = pl.multiple_of(j * TILE, TILE)
            there = pl.ds(begin, TILE)
            place = begin + iota((TILE, TILE), 1)
            allowed = (place >= low) & (place <= high)
            scores = [
                jnp.where(
                    allowed, dot_nt(heads_ref[h, here, :], k_ref[there, lanes_of(h // 2)]), LOWER
                )
                for h in heads
            ]
            tops = [
                jnp.maximum(state[2 * h], jnp.max(scores[h], axis=1, keepdims=True)) for h in heads
            ]
            shares = [jnp.exp(scores[h] - tops[h]) for h in heads]
            factors = [jnp.exp(state[2 * h] - tops[h]) for h in heads]
            sums = [
                state[2 * h + 1] * factors[h] + jnp.sum(shares[h], axis=1, keepdims=True)
                for h in heads
            ]
            more = [dot(shares[h].astype(BF16), v_ref[there, lanes_of(h // 2)]) for h in heads]
            for h in heads:
                acc_ref[h] = acc_ref[h] * factors[h] + more[h]
            return tuple(x for h in heads for x in (tops[h], sums[h]))

        first = (jnp.full((TILE, 1), LOW, F32), jnp.zeros((TILE, 1), F32))
        state = lax.fori_loop(
            meta_ref[0, 1 + t], total // TILE + t + 1, step, first * len(heads)
        )
        lane = iota((TILE, LANES), 1)
        logs = jnp.zeros((TILE, LANES), F32)
        for h in heads:
            logs = jnp.where(lane == h, state[2 * h] + jnp.log(state[2 * h + 1]), logs)
        log_ref[:, here] = logs.T[: log_ref.shape[0], :]
        for g in range(mine // LANES):
            left = acc_ref[2 * g] / state[4 * g + 1]
            right = acc_ref[2 * g + 1] / state[4 * g + 3]
            out = jnp.where(lane < HEAD_DIM, left, right)
            rows_ref[here, lanes_of(g)] = out
            tall_ref[lanes_of(g), here] = out.T
        return unused

    lax.fori_loop(0, total // TILE, tile, 0)

    def some(t, unused):
        at = pl.multiple_of(t * TILE, TILE)
        here = pl.ds(at, TILE)
        own_at = pl.ds(pl.multiple_of(core * half + at, TILE), TILE)
        sib_at = pl.ds(pl.multiple_of((1 - core) * half + at, TILE), TILE)
        all_ref[own_at, :] = rows_ref[own_at, :].astype(BF16)
        all_ref[sib_at, :] = rows_ref[sib_at, :].astype(BF16)
        own_ref[here, :] = rows_ref[own_at, :].astype(BF16)
        sib_ref[here, :] = rows_ref[sib_at, :].astype(BF16)
        return unused

    lax.fori_loop(0, half // TILE, some, 0)


def attend(meta, q, k, v, low):
    total, mine = q.shape
    heads = mine // HEAD_DIM
    outs = [
        shape((total // 2, mine), BF16),
        shape((total // 2, mine), BF16),
        shape((total, mine), BF16),
        shape((mine, total), F32),
        shape((-(-heads // 8) * 8, total), F32),
    ]
    return call(
        attend_body, "attend", outs, (meta, q, k, v, low), scalars=1,
        scratch=[pltpu.VMEM((heads, total, LANES), BF16), pltpu.VMEM((heads, TILE, LANES), F32),
                 pltpu.VMEM((total, mine), F32)],
    )


def fetch(pairs, sems):
    copies = [pltpu.make_async_copy(a, b, sems.at[i]) for i, (a, b) in enumerate(pairs)]
    for copy in copies:
        copy.start()
    return [copy.wait for copy in copies]


def both_rows(core, own, sib, rows_ref):
    half = own.shape[0]
    return [
        (own, rows_ref.at[pl.ds(pl.multiple_of(core * half, half), half), :]),
        (sib, rows_ref.at[pl.ds(pl.multiple_of((1 - core) * half, half), half), :]),
    ]


def attend_back_body(meta_ref, q_hbm, k_hbm, v_hbm, own_hbm, sib_hbm, wo_hbm, tall_hbm, log_ref,
                     lo_ref, gq_ref, gk_ref, gv_ref, rows_ref, heads_ref, grads_ref, delta_ref,
                     kt_ref, gqt_ref, gks_ref, gvs_ref, q_ref, k_ref, v_ref, wo_ref, tall_ref,
                     sems):
    total, mine = q_ref.shape
    heads = mine // HEAD_DIM
    core = meta_ref[0, 0]
    mine_at = pl.ds(pl.multiple_of(core * mine, mine), mine)
    waits = fetch(
        both_rows(core, own_hbm, sib_hbm, rows_ref)
        + [(wo_hbm.at[mine_at, :], wo_ref), (tall_hbm, tall_ref), (q_hbm, q_ref), (k_hbm, k_ref),
           (v_hbm, v_ref)],
        sems,
    )

    def clear(t, unused):
        here = pl.ds(pl.multiple_of(t * TILE, TILE), TILE)
        gks_ref[here, :] = jnp.zeros((TILE, mine), F32)
        gvs_ref[here, :] = jnp.zeros((TILE, mine), F32)
        return unused

    lax.fori_loop(0, 2 * total // TILE, clear, 0)
    gqt_ref[...] = jnp.zeros_like(gqt_ref)
    for wait in waits[:4]:
        wait()
    weights = wo_ref[...]

    def begin(t, unused):
        here = pl.ds(pl.multiple_of(t * TILE, TILE), TILE)
        grads = dot_nt(rows_ref[here, :], weights).astype(BF16)
        turned = grads.astype(F32).T * tall_ref[:, here]
        for h in range(heads):
            span = slice(h * HEAD_DIM, (h + 1) * HEAD_DIM)
            delta_ref[h : h + 1, here] = jnp.sum(turned[span, :], axis=0, keepdims=True)
        for g in range(mine // LANES):
            for h, part in enumerate(masked_heads(grads[:, lanes_of(g)])):
                grads_ref[2 * g + h, here, :] = part
        return unused

    lax.fori_loop(0, total // TILE, begin, 0)
    waits[4]()
    put_heads(heads_ref, q_ref)
    waits[5]()

    def turn(t, unused):
        here = pl.ds(pl.multiple_of(t * TILE, TILE), TILE)
        kt_ref[:, here] = flip(k_ref[here, :])
        return unused

    lax.fori_loop(0, 2 * total // TILE, turn, 0)
    waits[6]()

    def tile(t, unused):
        at = pl.multiple_of(t * TILE, TILE)
        here = pl.ds(at, TILE)
        low = lo_ref[:, here]
        high = total + at + iota((1, TILE), 1)

        logs = [log_ref[h : h + 1, here] for h in range(heads)]
        deltas = [delta_ref[h : h + 1, here] for h in range(heads)]

        def step(j, carry):
            begin = pl.multiple_of(j * TILE, TILE)
            there = pl.ds(begin, TILE)
            allowed = tile_mask(begin, low, high)
            every = range(heads)
            queries = [heads_ref[h, here, :] for h in every]
            grads = [grads_ref[h, here, :] for h in every]
            scores = [dot_nt(k_ref[there, lanes_of(h // 2)], queries[h]) for h in every]
            grad_soft = [dot_nt(v_ref[there, lanes_of(h // 2)], grads[h]) for h in every]
            soft = [jnp.exp(jnp.where(allowed, scores[h], LOWER) - logs[h]) for h in every]
            grad_scores = [(soft[h] * (grad_soft[h] - deltas[h])).astype(BF16) for h in every]
            soft = [s.astype(BF16) for s in soft]
            gv = [dot(soft[h], grads[h]) for h in every]
            gk = [dot(grad_scores[h], queries[h]) for h in every]
            gq = [
                dot(kt_ref[h * HEAD_DIM : (h + 1) * HEAD_DIM, there], grad_scores[h])
                for h in every
            ]
            for g in range(heads // 2):
                gvs_ref[there, lanes_of(g)] += gv[2 * g] + gv[2 * g + 1]
                gks_ref[there, lanes_of(g)] += gk[2 * g] + gk[2 * g + 1]
            for h in every:
                gqt_ref[h * HEAD_DIM : (h + 1) * HEAD_DIM, here] += gq[h]
            return carry

        return lax.fori_loop(meta_ref[0, 1 + t], total // TILE + t + 1, step, unused)

    lax.fori_loop(0, total // TILE, tile, 0)

    def finish_queries(t, unused):
        here = pl.ds(pl.multiple_of(t * TILE, TILE), TILE)
        gq_ref[here, :] = (gqt_ref[:, here].T * (HEAD_DIM**-0.5)).astype(BF16)
        return unused

    def finish_keys(t, unused):
        here = pl.ds(pl.multiple_of(t * TILE, TILE), TILE)
        gk_ref[here, :] = gks_ref[here, :].astype(BF16)
        gv_ref[here, :] = gvs_ref[here, :].astype(BF16)
        return unused

    lax.fori_loop(0, total // TILE, finish_queries, 0)
    lax.fori_loop(0, 2 * total // TILE, finish_keys, 0)


def attend_back(meta, q, k, v, own, sib, w_out, tall, logs, low):
    total, mine = q.shape
    width = own.shape[1]
    heads = mine // HEAD_DIM
    outs = [
        shape((total, mine), BF16),
        shape((2 * total, mine), BF16),
        shape((2 * total, mine), BF16),
    ]
    return call(
        attend_back_body, "attend_back", outs,
        (meta, q, k, v, own, sib, w_out, tall, logs, low), scalars=1,
        in_specs=[pl.BlockSpec(memory_space=pl.ANY)] * 7 + [pl.BlockSpec(memory_space=pltpu.VMEM)] * 2,
        scratch=[pltpu.VMEM((total, width), BF16), pltpu.VMEM((heads, total, LANES), BF16),
                 pltpu.VMEM((heads, total, LANES), BF16), pltpu.VMEM(logs.shape, F32),
                 pltpu.VMEM((mine, 2 * total), BF16), pltpu.VMEM((mine, total), F32),
                 pltpu.VMEM((2 * total, mine), F32), pltpu.VMEM((2 * total, mine), F32),
                 pltpu.VMEM(q.shape, BF16), pltpu.VMEM(k.shape, BF16), pltpu.VMEM(v.shape, BF16),
                 pltpu.VMEM((mine, width), BF16), pltpu.VMEM(tall.shape, F32),
                 pltpu.SemaphoreType.DMA((7,))],
    )


def dense_body(subs, sub, chip_ref, a_hbm, gq_hbm, gk_hbm, gv_hbm, all_hbm, own_hbm, sib_hbm,
               *refs):
    piece_refs = refs[:4]
    dense_ref, rows_ref, short_ref, long_ref, sems = refs[4:]
    unused, total, mine = short_ref.shape
    half = total // 2
    width = rows_ref.shape[1]
    lines = width // subs
    quarter = subs * sub
    core = chip_ref[0]
    own_at = pl.multiple_of(2 * total + core * half, half)
    sib_at = pl.multiple_of(2 * total + (1 - core) * half, half)
    waits = fetch(
        [(own_hbm, rows_ref.at[pl.ds(own_at, half), :]),
         (sib_hbm, rows_ref.at[pl.ds(sib_at, half), :]),
         (a_hbm, rows_ref.at[pl.ds(0, 2 * total), :]),
         (gq_hbm, short_ref.at[0]), (all_hbm, short_ref.at[1]),
         (gk_hbm, long_ref.at[0]), (gv_hbm, long_ref.at[1])],
        sems,
    )

    def put(kind, turned):
        for j in range(mine // LANES):
            block = turned[lanes_of(j), :].T.astype(BF16)
            for at in range(subs):
                first = pl.multiple_of(kind * quarter + at * sub + j * lines, 16)
                dense_ref[pl.ds(first, lines), :] = block[at * lines : (at + 1) * lines, :]

    def short(i, unused):
        rows = rows_ref[pl.ds(pl.multiple_of((1 + i) * total, total), total), :]
        put(3 * i, dot_tn(short_ref[i], rows))
        return unused

    def long(i, unused):
        put(1 + i, dot_tn(long_ref[i], rows_ref[: 2 * total, :]))
        return unused

    for wait in waits[:5]:
        wait()
    lax.fori_loop(0, 2, short, 0)
    waits[5]()
    waits[6]()
    lax.fori_loop(0, 2, long, 0)
    spare = sub - mine // LANES * lines
    if spare:
        for at in range(4 * subs):
            dense_ref[(at + 1) * sub - spare : (at + 1) * sub, :] = jnp.zeros((spare, LANES), BF16)
    for p in range(2):
        side = chip_ref[1 + p]
        for r, which in enumerate((side, 1 - side)):
            for at in range(subs):
                from_at = pl.multiple_of((2 * p + which) * quarter + at * sub, 16)
                to_at = pl.multiple_of((at ^ chip_ref[3 + p]) * sub, 16)
                piece_refs[2 * p + r][pl.ds(to_at, sub), :] = dense_ref[pl.ds(from_at, sub), :]


def dense_pieces(chip, a, gq, gk, gv, attn_all, own, sib, subs, sub):
    return call(
        functools.partial(dense_body, subs, sub), "dense",
        [shape((subs * sub, LANES), BF16)] * 4,
        (chip, a, gq, gk, gv, attn_all, own, sib), scalars=1,
        in_specs=[pl.BlockSpec(memory_space=pl.ANY)] * 7,
        scratch=[pltpu.VMEM((4 * subs * sub, LANES), BF16),
                 pltpu.VMEM((3 * gq.shape[0], a.shape[1]), BF16),
                 pltpu.VMEM((2, *gq.shape), BF16), pltpu.VMEM((2, *gk.shape), BF16),
                 pltpu.SemaphoreType.DMA((7,))],
    )


def lift_body(parts, capacity, core_ref, own_ref, other_ref, w_ref, x_ref, norm_ref, slot_ref,
              resid_ref, *out_refs):
    mine = own_ref.shape[1]
    core = core_ref[0]
    own_at = pl.ds(pl.multiple_of(core * mine, mine), mine)
    other_at = pl.ds(pl.multiple_of((1 - core) * mine, mine), mine)
    *out_refs, rows_ref = out_refs

    def some(t, unused):
        here = pl.ds(pl.multiple_of(t * TILE, TILE), TILE)
        more = dot(own_ref[here, :], w_ref[own_at, :]) + dot(other_ref[here, :], w_ref[other_at, :])
        resid = x_ref[here, :].astype(F32) + more
        resid_ref[here, :] = resid
        normed, scale = norm_rows(resid)
        rows_ref[here, :] = (normed * vector(norm_ref, 2) + vector(norm_ref, 3)).astype(BF16)
        return unused

    lax.fori_loop(0, own_ref.shape[0] // TILE, some, 0)
    slot = slot_ref[...]
    for k in range(parts):
        chosen = one_hot(slot - k * capacity, capacity)
        out_refs[k][...] = dot_tn(chosen, rows_ref[...]).astype(BF16)


def lift(core, own, other, w_out, x, norms, slot, parts, capacity):
    count, width = x.shape
    outs = [shape((count, width), F32)] + [shape((capacity, width), BF16)] * parts
    return call(
        functools.partial(lift_body, parts, capacity), "lift", outs,
        (core, own, other, w_out, x, norms, slot), scratch=[pltpu.VMEM((count, width), BF16)],
        scalars=1, flops=2 * count * width * (width + parts * capacity),
    )


GATE_A = math.sqrt(2.0 / math.pi)
GATE_B = 0.044715


def expert_body(sub, rows_ref, grad_ref, up_ref, down_ref, tall_ref, pre_ref, back_ref, out_ref,
                turned_ref, back_acc, out_acc):
    step = pl.program_id(0)

    @pl.when(step == 0)
    def _():
        back_acc[...] = jnp.zeros_like(back_acc)
        out_acc[...] = jnp.zeros_like(out_acc)
        turned_ref[...] = flip(rows_ref[...])

    parts = [slice(s * sub, (s + 1) * sub) for s in range(down_ref.shape[0] // sub)]
    pres = [dot(rows_ref[...], up_ref[:, part]) for part in parts]
    grads = [dot_nt(grad_ref[...], down_ref[part, :]) for part in parts]
    hids, slopes = [], []
    for pre in pres:
        square = pre * pre
        bend = jnp.tanh(GATE_A * (pre + GATE_B * (square * pre)))
        half = 0.5 + 0.5 * bend
        hids.append(pre * half)
        slopes.append(
            half + (pre * (1.0 - bend * bend)) * (0.5 * GATE_A + (1.5 * GATE_A * GATE_B) * square)
        )
    low = jnp.concatenate([(g * s).astype(BF16) for g, s in zip(grads, slopes)], axis=1)
    back_acc[...] += dot_nt(low, up_ref[...])
    out_acc[...] += dot(jnp.concatenate([h.astype(BF16) for h in hids], axis=1), down_ref[...])
    pre_ref[...] = low
    for part, hid in zip(parts, hids):
        tall_ref[part, :] = hid.T.astype(BF16)

    @pl.when(step == pl.num_programs(0) - 1)
    def _():
        back_ref[...] = back_acc[...].astype(BF16)
        out_ref[...] = out_acc[...].astype(BF16)


def expert(rows, grads, w_up, w_down, sub=256):
    count, width = rows.shape
    hidden = w_up.shape[1]
    block = width
    const = pl.BlockSpec((count, width), lambda j: (0, 0))
    return call(
        functools.partial(expert_body, sub), "expert",
        [shape((hidden, count), BF16), shape((count, hidden), BF16), shape((count, width), BF16),
         shape((count, width), BF16), shape((width, count), BF16)],
        (rows, grads, w_up, w_down), grid=(hidden // block,),
        in_specs=[const, const, pl.BlockSpec((width, block), lambda j: (0, j)),
                  pl.BlockSpec((block, width), lambda j: (j, 0))],
        out_specs=[pl.BlockSpec((block, count), lambda j: (j, 0)),
                   pl.BlockSpec((count, block), lambda j: (0, j)), const, const,
                   pl.BlockSpec((width, count), lambda j: (0, 0))],
        scratch=[pltpu.VMEM((count, width), F32)] * 2,
    )


def expert_grad_body(parts, subs, chip_ref, *refs):
    turned, grads, talls, pres = (refs[parts * t : parts * (t + 1)] for t in range(4))
    *outs, held_ref, sems = refs[4 * parts :]
    width = held_ref.shape[2]
    lines = width // subs
    step = pl.program_id(0)
    steps = len(outs)
    slot = step % 2

    def copy(t, at):
        return pltpu.make_async_copy(held_ref.at[at], outs[t], sems.at[at])

    @pl.when(step >= 2)
    def _():
        copy(0, slot).wait()

    def product(left, right):
        out = None
        for a, b in zip(left, right):
            more = dot(a[...], b[...])
            out = more if out is None else out + more
        return out.astype(BF16)

    half = steps // 2
    side, mask = chip_ref[1 + step % half], chip_ref[3 + step % half]
    pairs = ((product(turned, pres), side == 0), (product(talls, grads), side == 1))
    for value, stays in pairs:
        base = jnp.where(stays, width, 0)
        for at in range(subs):
            first = pl.multiple_of(base + (at ^ mask) * lines, 16)
            held_ref[slot, pl.ds(first, lines), :] = value[at * lines : (at + 1) * lines, :]

    for t in range(steps):

        @pl.when(step == t)
        def _(t=t):
            copy(t, t % 2).start()

    @pl.when(step == steps - 1)
    def _():
        copy(0, 0).wait()
        copy(0, 1).wait()


def expert_grad(chip, turned, grads, talls, pres, subs):
    parts = len(grads)
    count, width = grads[0].shape
    blocks = talls[0].shape[0] // width
    half = blocks // 2

    def column(i, m):
        return jnp.where(i < half, (1 - m[0]) * half, m[0] * half - half) + i

    const = lambda dims: pl.BlockSpec(dims, lambda i, m: (0, 0))
    return call(
        functools.partial(expert_grad_body, parts, subs), "expert_grad",
        [shape((2 * width, width), BF16)] * blocks,
        (chip, *turned, *grads, *talls, *pres), grid=(blocks,), scalars=1,
        in_specs=[const((width, count))] * parts + [const((count, width))] * parts
        + [pl.BlockSpec((width, count), lambda i, m: (column(i, m), 0))] * parts
        + [pl.BlockSpec((count, width), lambda i, m: (0, column(i, m)))] * parts,
        out_specs=[pl.BlockSpec(memory_space=pl.ANY)] * blocks,
        scratch=[pltpu.VMEM((2, 2 * width, width), BF16), pltpu.SemaphoreType.DMA((2,))],
    )


def widen_body(skip, meta_ref, *refs):
    pairs, (up_out, down_out) = refs[:4], refs[4 + skip :]
    second = pl.program_id(0) >= pl.num_programs(0) // 2
    first = meta_ref[1 + pl.program_id(0) // (pl.num_programs(0) // 2)] == 0
    mine = jnp.where(second, pairs[2][...], pairs[0][...])
    theirs = jnp.where(second, pairs[3][...], pairs[1][...])
    up_out[...] = jnp.where(first, mine, theirs).astype(F32)
    down_out[...] = jnp.where(first, theirs, mine).astype(F32)


def widen(core, sides, masks, mine, theirs, made, hidden, subs):
    width = mine[0].shape[1]
    rows = width // subs
    meta = jnp.stack([core, *sides, *masks]).astype(jnp.int32)

    def index(p):
        def at(i, m):
            here = jnp.clip(i - p * subs, 0, subs - 1)
            return (here ^ m[3 + p], 0)

        return at

    blocks = [pl.BlockSpec((rows, width), index(p)) for p in (0, 0, 1, 1)]
    column = lambda i, m: 2 * m[0] + i // subs
    return call(
        functools.partial(widen_body, len(made)), "widen",
        [shape((width, hidden), F32), shape((hidden, width), F32)],
        (meta, mine[0], theirs[0], mine[1], theirs[1], *made), grid=(2 * subs,), scalars=1,
        in_specs=blocks + [pl.BlockSpec(memory_space=pl.ANY)] * len(made),
        out_specs=[pl.BlockSpec((rows, width), lambda i, m: (i % subs, column(i, m))),
                   pl.BlockSpec((rows, width), lambda i, m: (column(i, m) * subs + i % subs, 0))],
        aliases={5: 0, 6: 1} if made else None,
    )


def collect(slot, part_refs):
    total = None
    for k, ref in enumerate(part_refs):
        capacity = ref.shape[0]
        more = dot(one_hot(slot - k * capacity, capacity), ref[...])
        total = more if total is None else total + more
    return total


def lower_body(parts, slot_ref, resid_ref, cot_ref, norm_ref, *refs):
    grads = collect(slot_ref[...], refs[:parts])
    gr_ref, low_ref, gain_out, bias_out = refs[parts:]
    normed, scale = norm_rows(resid_ref[...])

    @pl.when(pl.program_id(0) == 0)
    def _():
        gain_out[...] = jnp.zeros_like(gain_out)
        bias_out[...] = jnp.zeros_like(bias_out)

    gain_out[...] += jnp.sum(grads * normed, axis=0, keepdims=True)
    bias_out[...] += jnp.sum(grads, axis=0, keepdims=True)
    gr = cot_ref[...].astype(F32) + norm_back(grads * vector(norm_ref, 2), normed, scale)
    gr_ref[...] = gr
    low_ref[...] = gr.astype(BF16)


def row_specs(dims, *whole):
    return [pl.BlockSpec((TILE, d), lambda i: (i, 0)) for d in dims] + [
        pl.BlockSpec(w.shape, lambda i: (0, 0)) for w in whole
    ]


def lower(slot, resid, cot, norms, back):
    parts = len(back)
    count, width = resid.shape
    outs = [shape((count, width), F32), shape((count, width), BF16),
            shape((1, width), F32), shape((1, width), F32)]
    return call(
        functools.partial(lower_body, parts), "lower", outs, (slot, resid, cot, norms, *back),
        grid=(count // TILE,), in_specs=row_specs((1, width, width), norms, *back),
        out_specs=row_specs((width, width), outs[2], outs[3]),
    )


def finish_body(slot_ref, resid_ref, *refs):
    refs[-1][...] = (resid_ref[...] + collect(slot_ref[...], refs[:-1])).astype(BF16)


def finish(slot, resid, parts):
    count, width = resid.shape
    return call(
        finish_body, "finish", shape(resid.shape, BF16), (slot, resid, *parts),
        grid=(count // TILE,), in_specs=row_specs((1, width), *parts),
        out_specs=row_specs((width,))[0],
    )


def project_back_body(half, core_ref, own_ref, sib_ref, hal_ref, has_ref, gq_ref, gk_ref, gv_ref,
                      wq_ref, wk_ref, wv_ref, keep_ref, send_ref, halo_ref, gain_ref, bias_ref):
    step = pl.program_id(0)
    rows = jnp.where(
        step < 2 * half,
        jnp.where(step < half, own_ref[...], sib_ref[...]),
        jnp.where(step < 3 * half, hal_ref[...], has_ref[...]),
    )
    normed, unused = norm_rows(rows.astype(F32))
    here = step < 2 * half
    ga = dot_nt(gk_ref[...], wk_ref[...]) + dot_nt(gv_ref[...], wv_ref[...])
    gq = jnp.where(here, gq_ref[...], jnp.zeros_like(gq_ref))
    ga = ga + dot_nt(gq, wq_ref[...])

    @pl.when(step == 0)
    def _():
        gain_ref[...] = jnp.zeros_like(gain_ref)
        bias_ref[...] = jnp.zeros_like(bias_ref)

    gain_ref[...] += jnp.sum(ga * normed, axis=0, keepdims=True)
    bias_ref[...] += jnp.sum(ga, axis=0, keepdims=True)

    @pl.when(step < half)
    def _():
        keep_ref[...] = ga

    @pl.when((step // half) % 2 == 1)
    def _():
        send_ref[...] = ga.astype(BF16)

    @pl.when(step // half == 2)
    def _():
        halo_ref[...] = ga


def project_back(core, own, sib, hal, has, gq, gk, gv, w_qkv):
    count, width = own.shape
    mine = gq.shape[1]
    half = count // TILE

    def at(t):
        return lambda i, c: (jnp.clip(i - t * half, 0, half - 1), 0)

    def place(i, c):
        return jnp.where(i < 2 * half, 2 * half, 0) + (((i // half) % 2) ^ c[0]) * half + i % half

    def sent(i, c):
        late = half + jnp.clip(i - 3 * half, 0, half - 1)
        return (jnp.where(i < 2 * half, jnp.clip(i - half, 0, half - 1), late), 0)

    row = pl.BlockSpec((1, width), lambda i, c: (0, 0))
    in_specs = [pl.BlockSpec((TILE, width), at(t)) for t in range(4)] + [
        pl.BlockSpec((TILE, mine), lambda i, c: (jnp.maximum(place(i, c) - 2 * half, 0), 0)),
        pl.BlockSpec((TILE, mine), lambda i, c: (place(i, c), 0)),
        pl.BlockSpec((TILE, mine), lambda i, c: (place(i, c), 0)),
    ] + [
        pl.BlockSpec((width, mine), functools.partial(lambda t, i, c: (0, 2 * t + c[0]), t))
        for t in range(3)
    ]
    return call(
        functools.partial(project_back_body, half), "project_back",
        [shape((count, width), F32), shape((2 * count, width), BF16), shape((count, width), F32),
         shape((1, width), F32), shape((1, width), F32)],
        (core, own, sib, hal, has, gq, gk, gv, w_qkv, w_qkv, w_qkv),
        grid=(4 * half,), in_specs=in_specs, scalars=1,
        out_specs=[pl.BlockSpec((TILE, width), at(0)), pl.BlockSpec((TILE, width), sent),
                   pl.BlockSpec((TILE, width), at(2)), row, row],
        flops=20 * count * width * mine,
    )


def close_body(x_ref, gr_ref, keep_ref, near_ref, far_ref, norm_ref, out_ref):
    ga = keep_ref[...] + near_ref[...].astype(F32) + far_ref[...].astype(F32)
    normed, scale = norm_rows(x_ref[...].astype(F32))
    out_ref[...] = gr_ref[...] + norm_back(ga * vector(norm_ref, 0), normed, scale)


def close(x, gr, keep, near, far, norms):
    count, width = x.shape
    block = pl.BlockSpec((TILE, width), lambda i: (i, 0))
    return call(
        close_body, "close", shape((count, width), F32), (x, gr, keep, near, far, norms),
        grid=(count // TILE,),
        in_specs=[block] * 5 + [pl.BlockSpec(norms.shape, lambda i: (0, 0))], out_specs=block,
    )


def swap(block, axis, distance):
    return lax.ppermute(block, axis, [(i, i ^ distance) for i in range(lax.axis_size(axis))])


def trade(block, axis):
    return lax.all_to_all(block, axis, split_axis=0, concat_axis=0, tiled=True)


def shift(block, axis, distance):
    size = lax.axis_size(axis)
    route = [(i, i + distance) for i in range(size) if 0 <= i + distance < size]
    return lax.ppermute(block, axis, route)


def total(terms):
    return sum(t.astype(F32) for t in terms).astype(BF16)


def add(a, b):
    return total([a, b])


def at_index(block, index):
    return lax.dynamic_index_in_dim(block, index, 0, keepdims=False)


def scatter_steps(pieces, orders):
    pairs = list(pieces)
    for s in range(len(orders[0])):
        arrived = yield [(goes, "seq", bits[s]) for (stays, goes), bits in zip(pairs, orders)]
        terms = [stays + [got] for (stays, goes), got in zip(pairs, arrived)]
        if s + 1 < len(orders[0]):
            half = terms[0][0].shape[0] // 2
            pairs = [
                ([total([t[half:] for t in terms_p])], total([t[:half] for t in terms_p]))
                for terms_p in terms
            ]
    return [total(terms_p) for terms_p in terms]


def gather_steps(parts, orders):
    parts = list(parts)
    for s in reversed(range(1, len(orders[0]))):
        arrived = yield [(part, "seq", bits[s]) for part, bits in zip(parts, orders)]
        parts = [jnp.concatenate([got, part], axis=0) for got, part in zip(arrived, parts)]
    return parts


def dense_steps(pieces, orders):
    sources = lax.axis_size("exp")
    parts = yield from scatter_steps(pieces, orders)
    joined = jnp.stack([p.reshape(sources, -1, LANES) for p in parts], axis=1)
    (got,) = yield [(joined, "exp", 0)]
    own = jnp.sum(got.astype(F32), axis=0).astype(BF16)
    (got,) = yield [(jnp.broadcast_to(own, (sources, *own.shape)), "exp", 0)]
    parts = [got[:, p].reshape(-1, LANES) for p in range(len(orders))]
    return (yield from gather_steps(parts, orders))


def expert_steps(pieces, orders):
    parts = yield from scatter_steps(pieces, orders)
    return (yield from gather_steps(parts, orders))


def one_step(sends):
    return (yield sends)


def across(parts, orders):
    return Stream(one_step([(part, "seq", bits[0]) for part, bits in zip(parts, orders)]))


def beside(parts):
    return Stream(one_step([(part, "seq", 1) for part in parts]))


def small_steps(value, hops):
    for hop in hops:
        (got,) = yield [(value, *hop)]
        value = value + got
    return value


class Stream:
    def __init__(self, steps):
        self.steps = steps
        self.result = None
        self.sent = []
        self.go(None)

    def go(self, arrived):
        try:
            sends = self.steps.send(arrived)
        except StopIteration as stop:
            self.sent, self.raw, self.result = [], [], stop.value
        else:
            self.raw = [send[0] for send in sends]
            self.sent = [swap(*send) if send[2] else trade(*send[:2]) for send in sends]


def meet(streams, others=()):
    streams = [stream for stream in streams if stream.sent]
    arrived, others = lax.optimization_barrier(([stream.sent for stream in streams], others))
    before = []
    for stream, got in zip(streams, arrived):
        stream.go(after(got, before) if before else got)
        before = before + stream.raw
    return others


def spread_columns_body(cols, chip_ref, *refs):
    out_ref = refs[-1]
    first = chip_ref[0] == 0
    own, sib = refs[:4], refs[4:8]
    picks = [
        (0, chip_ref[1] == 0, 0, 1),
        (1, chip_ref[1] == 1, 0, 1),
        (2, chip_ref[2] == 0, 2, 3),
    ]
    for kind, mine, here, there in picks:
        for j in range(cols):
            a, b = (jnp.where(mine, t[here][0, j], t[there][0, j]).astype(F32) for t in (own, sib))
            left = 2 * kind * cols + j
            out_ref[:, lanes_of(left)] = jnp.where(first, a, b)
            out_ref[:, lanes_of(left + cols)] = jnp.where(first, b, a)


def spread_rows_body(chip_ref, *refs):
    out_ref = refs[-1]
    own = pl.program_id(0) == chip_ref[0]
    mine = chip_ref[2] == 1
    subs, cols, lines, unused = refs[0].shape
    for at in range(subs):
        from_at = at ^ chip_ref[4]
        for j in range(cols):
            a, b = (
                jnp.where(mine, refs[t][from_at, j], refs[t + 1][from_at, j]) for t in (0, 2)
            )
            out_ref[lanes_of(j), at * lines : (at + 1) * lines] = (
                jnp.where(own, a, b).astype(F32).T
            )


def spread(chip, own, sib, width, mine, subs):
    cols = mine // LANES
    lines = width // subs
    block = math.gcd(lines, 192)

    def view(t):
        return t.reshape(subs, -1, LANES)[:, : cols * lines].reshape(subs, cols, lines, LANES)

    def part(p):
        def index(i, m):
            return ((i * block // lines) ^ m[3 + p], 0, i % (lines // block), 0)

        return pl.BlockSpec((1, cols, block, LANES), index)

    parts = [[view(t) for pair in side for t in pair] for side in (own, sib)]
    grad_qkv = call(
        functools.partial(spread_columns_body, cols), "spread_columns",
        shape((width, 3 * width), F32), (chip, *parts[0], *parts[1]), grid=(width // block,),
        scalars=1, in_specs=[part(0), part(0), part(1), part(1)] * 2,
        out_specs=pl.BlockSpec((block, 3 * width), lambda i, m: (i, 0)),
    )
    whole = pl.BlockSpec((subs, cols, lines, LANES), lambda i, m: (0, 0, 0, 0))
    grad_out = call(
        spread_rows_body, "spread_rows", shape((width, width), F32),
        (chip, *parts[0][2:], *parts[1][2:]), grid=(2,), scalars=1, in_specs=[whole] * 4,
        out_specs=pl.BlockSpec((mine, width), lambda i, m: (i, 0)),
    )
    return grad_qkv, grad_out


def on_device(
    layer_input,
    token_ids,
    segment_ids,
    hash_table,
    first_gain,
    first_bias,
    second_gain,
    second_bias,
    w_qkv,
    w_out,
    w_up,
    w_down,
    cotangent,
):
    x = layer_input[0]
    cot = cotangent[0]
    local_len, width = x.shape
    mine = width // 2
    sources = lax.axis_size("exp")
    ring = lax.axis_size("seq")
    capacity = 2 * local_len // sources
    seq_at = lax.axis_index("seq")
    exp_at = lax.axis_index("exp")
    core = (seq_at % 2).astype(jnp.int32)
    core_arg = core.reshape(1)
    norms = jnp.concatenate([first_gain, first_bias, second_gain, second_bias])
    norms = norms.reshape(-1, LANES)
    up, down = w_up[0], w_down[0]

    hal = shift(x, "seq", 2)
    sib = swap(x, "seq", 1)

    place = exp_at.astype(jnp.int32).reshape(1)
    at = jnp.stack([exp_at, core, seq_at // 2]).astype(jnp.int32)
    lines = -(-hash_table.shape[0] // (8 * LANES)) * 8
    table = jnp.pad(hash_table, (0, lines * LANES - hash_table.shape[0])).reshape(lines, LANES)
    docs = 2 * ring * local_len // DOC_MOST
    slot, low, low_tall, meta, *grad_out = route(
        at, token_ids, table, cot, segment_ids, sources, capacity, docs
    )
    grad_in = [grad_out[0]] + [swap(grad_out[k], "exp", k) for k in range(1, sources)]

    *made, q = project(core_arg, x, after(sib, slot), norms, w_qkv, None)
    hal = after(hal, q)
    has = swap(hal, "seq", 1)
    a, k, v = project(core_arg, hal, has, norms, w_qkv, made)
    attn_own, attn_give, attn_all, attn_tall, logs = attend(meta, q, k, v, low_tall)
    attn_other = swap(attn_give, "seq", 1)
    resid, *rows_out = lift(
        core_arg, attn_own, after(attn_other, grad_in), w_out, x, norms, slot, sources, capacity
    )
    rows_in = [rows_out[0]] + [swap(rows_out[k], "exp", k) for k in range(1, sources)]
    talls, pres, backs, outs, turned = [], [], [], [], []
    for k_at in range(sources):
        tall, pre, back, out, turn = expert(rows_in[k_at], grad_in[k_at], up, down)
        talls.append(tall)
        pres.append(pre)
        outs.append(out)
        turned.append(turn)
        backs.append(back if k_at == 0 else swap(back, "exp", k_at))
        if k_at + 1 < sources:
            rows_in[k_at + 1] = after(rows_in[k_at + 1], back)
    bits = [1 << b for b in range(1, ring.bit_length() - 1)]
    orders = [bits, bits[::-1]]
    sides = [(seq_at // o[0]) % 2 for o in orders]
    subs = ring // 4
    masks = [
        sum((1 - (seq_at // bit) % 2) << (len(o) - 2 - at) for at, bit in enumerate(o[1:]))
        for o in orders
    ]
    chip = jnp.stack([core, *sides, *masks]).astype(jnp.int32)

    turned, backs[:-2] = lax.optimization_barrier((turned, backs[:-2]))
    blocks = expert_grad(chip, turned, grad_in, talls, pres, subs)
    given, kept = blocks[:2], blocks[2:]
    given, backs[-2] = lax.optimization_barrier((given, backs[-2]))
    given, backs[-1] = lax.optimization_barrier((given, backs[-1]))
    got = [swap(t, "seq", 1) for t in given]
    gr, gattn, gain_two_grad, bias_two_grad = lower(slot, resid, cot, norms, backs)
    got = after(got, gattn)
    goes = [add(kept[p][:width], got[p][:width]) for p in range(2)]
    stays = [[kept[p][width:], got[p][width:]] for p in range(2)]
    experts = Stream(expert_steps(list(zip(stays, goes)), orders))
    outs = after(outs, goes)
    returned = [outs[0]] + [swap(outs[k], "exp", k) for k in range(1, sources)]
    gattn_sib = swap(gattn, "seq", 1)
    unit = sources * 16
    sub = -(-(mine // LANES * width // subs) // unit) * unit
    gq, gk, gv = attend_back(
        meta, q, k, v, gattn, after(gattn_sib, goes), w_out, attn_tall, logs, low
    )
    pieces = dense_pieces(chip, a, gq, gk, gv, attn_all, gattn, gattn_sib, subs, sub)
    pieces, returned = lax.optimization_barrier((pieces, returned))
    dense = Stream(
        dense_steps([([pieces[0]], pieces[1]), ([pieces[2]], pieces[3])], orders)
    )
    (gq,) = meet([experts], (after(gq, pieces),))
    keep, give, halo, gain_one_grad, bias_one_grad = project_back(
        core_arg, x, sib, hal, has, gq, gk, gv, w_qkv
    )
    small = jnp.concatenate([gain_one_grad, bias_one_grad, gain_two_grad, bias_two_grad], axis=0)
    (give,) = meet([dense, experts], (give,))
    near = swap(give, "seq", 1)
    (near,) = meet([dense], (near,))
    for rest in range(len(bits) - 2):
        meet([dense, experts])
    far = shift(add(halo, near[local_len:]), "seq", -2)
    hops = [("seq", bit) for bit in bits + [1]]
    hops += [("exp", 1 << b) for b in range(sources.bit_length() - 1)]
    small = Stream(small_steps(small, hops))
    layer_output = finish(slot, resid, returned)
    (layer_output,) = meet([dense, experts, small], (layer_output,))
    for rest in range(len(bits) - 2):
        meet([experts])
    own_parts = experts.result
    other_chip = across(own_parts, orders)
    other_core = beside(after(own_parts, layer_output))
    meet([dense, other_chip, other_core, small])
    other_both = beside(other_chip.result)
    hidden = down.shape[0]
    made = widen(core, sides, masks, own_parts, other_chip.result, (), hidden, subs)
    while dense.result is None:
        made = meet([dense, other_both, small], made)
    own_dense = dense.result
    dense_chip, dense_core = across(own_dense, orders), beside(own_dense)
    made = widen(
        1 - core, sides, masks, other_core.result, other_both.result, made, hidden, subs
    )
    grad_w_up, grad_w_down = meet([dense_chip, dense_core, small], made)
    dense_both = beside(dense_chip.result)
    meet([dense_both, small])
    while small.sent:
        small.go(small.sent)
    grad_w_qkv, grad_w_out = spread(
        chip, list(zip(own_dense, dense_chip.result)),
        list(zip(dense_core.result, dense_both.result)), width, mine, subs,
    )
    grad_input = close(x, gr, keep, near, after(far, grad_w_qkv), norms)
    small = small.result
    return (
        layer_output[None],
        grad_input[None],
        grad_w_qkv,
        grad_w_out,
        small[0],
        small[1],
        small[2],
        small[3],
        grad_w_up[None],
        grad_w_down[None],
    )


def solution(mesh):
    in_specs = (
        P("exp", "seq", None),
        P("exp", "seq"),
        P("exp", None),
        P(),
        P(),
        P(),
        P(),
        P(),
        P(),
        P(),
        P("exp", None, None),
        P("exp", None, None),
        P("exp", "seq", None),
    )
    out_specs = (
        P("exp", "seq", None),
        P("exp", "seq", None),
        P(),
        P(),
        P(),
        P(),
        P(),
        P(),
        P("exp", None, None),
        P("exp", None, None),
    )
    return jax.shard_map(
        on_device, mesh=mesh, in_specs=in_specs, out_specs=out_specs, check_vma=False
    )
```

profile of v0, /device:TPU:0, one launch (start us, length us, event | category | flops | bytes accessed | tf_op | source)
XLA Modules:
  0.0 348.6 jit_solution(12189578509606275378)
XLA Ops:
  7.6 5.0 %route.1 = (s32[512,1]{1,0:T(8,128)}, s32[1,1024]{1,0:T(1,128)}, s32[1024,1]{1,0:T(8,128)}, s32[1,128]{1,0:T(1,128)}, bf16[256,768]{1,0:T(8,128)(2,1)}, /*index=...) custom-call(s32[3]{0:T(128)} %pad_add_fusion.at_ref, s32[1,512]{1,0:T(1,128)} %ids_ref.1, ...), custom_call_target="tpu_custom_call" | custom-call | flops 1 | bytes 1 | tf_op jit(solution)/shard_map/route/pallas_call | solution.py:74
  14.8 7.6 %project.2 = (bf16[2048,768]{1,0:T(8,128)(2,1)}, bf16[2048,384]{1,0:T(8,128)(2,1)}, bf16[2048,384]{1,0:T(8,128)(2,1)}, bf16[1024,384]{1,0:T(8,128)(2,1)}) custom-call(s32[1]{0:T(128)} %bitcast.core_ref, bf16[512,768]{1,0:T(8,128)(2,1)} %bitcast.48, bf16[512,768]{1,0:T(8,128)(2,1)} %copy-done.5, f32[24,128]{1,0:T(8,128)} %pad_maximum_fusion.5.norm_ref, ...), custom_call_target="tpu_custom_call" | custom-call | flops 1 | bytes 1 | tf_op jit(solution)/shard_map/project/pallas_call | solution.py:74
  28.6 6.5 %project.3 = (bf16[2048,768]{1,0:T(8,128)(2,1)}, bf16[2048,384]{1,0:T(8,128)(2,1)}, bf16[2048,384]{1,0:T(8,128)(2,1)}) custom-call(s32[1]{0:T(128)} %bitcast.core_ref, bf16[512,768]{1,0:T(8,128)(2,1)} %copy-done.3, bf16[512,768]{1,0:T(8,128)(2,1)} %copy-done.4, ...), custom_call_target="tpu_custom_call", output_to_operand_aliasing={{0}: (7, {}), {1}: (8, {}), {2}: (9, {})} | custom-call | flops 1 | bytes 1 | tf_op jit(solution)/shard_map/project/pallas_call | solution.py:74
  35.1 19.0 %attend.1 = (bf16[512,384]{1,0:T(8,128)(2,1)}, bf16[512,384]{1,0:T(8,128)(2,1)}, bf16[1024,384]{1,0:T(8,128)(2,1)}, f32[384,1024]{1,0:T(8,128)}, f32[8,1024]{1,0:T(8,128)}) custom-call(s32[1,128]{1,0:T(1,128)} %get-tuple-element.173.meta_ref, bf16[1024,384]{1,0:T(8,128)(2,1)} %get-tuple-element.167.q_ref.q_hbm, ...), custom_call_target="tpu_custom_call" | custom-call | flops 1 | bytes 1 | tf_op jit(solution)/shard_map/attend/pallas_call | solution.py:74
  56.8 5.8 %lift.1 = (f32[512,768]{1,0:T(8,128)}, bf16[256,768]{1,0:T(8,128)(2,1)}, bf16[256,768]{1,0:T(8,128)(2,1)}, bf16[256,768]{1,0:T(8,128)(2,1)}, bf16[256,768]{1,0:T(8,128)(2,1)}) custom-call(s32[1]{0:T(128)} %bitcast.core_ref, bf16[512,384]{1,0:T(8,128)(2,1)} %get-tuple-element.177.own_ref, bf16[512,384]{1,0:T(8,128)(2,1)} %copy-done.34, ...), custom_call_target="tpu_custom_call" | custom-call | flops 1 | bytes 1 | tf_op jit(solution)/shard_map/lift/pallas_call | solution.py:74
  62.6 6.9 %collective-permute-start.7 = (bf16[256,768]{1,0:T(8,128)(2,1)}, bf16[256,768]{1,0:T(8,128)(2,1)S(1)}, u32[]{:S(2)}, u32[]{:S(2)}) collective-permute-start(bf16[256,768]{1,0:T(8,128)(2,1)} %get-tuple-element.187), channel_id=1, source_target_pairs={{0,1},{1,0},{2,3},{3,2},{4,5},{5,4},{6,7},{7,6},{8,9},{9,8},{10,11... | collective-permute-start | bytes 1179656 | tf_op jit(solution)/shard_map/ppermute | solution.py:889
  72.0 10.1 %expert.4 = (bf16[3072,256]{1,0:T(8,128)(2,1)}, bf16[256,3072]{1,0:T(8,128)(2,1)}, bf16[256,768]{1,0:T(8,128)(2,1)}, bf16[256,768]{1,0:T(8,128)(2,1)}, bf16[768,256]{1,0:T(8,128)(2,1)}) custom-call(bf16[256,768]{1,0:T(8,128)(2,1)} %get-tuple-element.185.rows_ref, bf16[256,768]{1,0:T(8,128)(2,1)} %get-tuple-element.179.grad_ref.refs_4_, ...), custom_call_target="tpu_custom_call" | custom-call | flops 1 | bytes 1 | tf_op jit(solution)/shard_map/expert/pallas_call | solution.py:74
  86.6 10.1 %expert.5 = (bf16[3072,256]{1,0:T(8,128)(2,1)}, bf16[256,3072]{1,0:T(8,128)(2,1)}, bf16[256,768]{1,0:T(8,128)(2,1)}, bf16[256,768]{1,0:T(8,128)(2,1)}, bf16[768,256]{1,0:T(8,128)(2,1)}) custom-call(bf16[256,768]{1,0:T(8,128)(2,1)} %copy-done.30, bf16[256,768]{1,0:T(8,128)(2,1)} %copy-done.17, bf16[768,3072]{1,0:T(8,128)(2,1)} %bitcast.39, ...), custom_call_target="tpu_custom_call" | custom-call | flops 1 | bytes 1 | tf_op jit(solution)/shard_map/expert/pallas_call | solution.py:74
  100.3 10.2 %expert.6 = (bf16[3072,256]{1,0:T(8,128)(2,1)}, bf16[256,3072]{1,0:T(8,128)(2,1)}, bf16[256,768]{1,0:T(8,128)(2,1)}, bf16[256,768]{1,0:T(8,128)(2,1)}, bf16[768,256]{1,0:T(8,128)(2,1)}) custom-call(bf16[256,768]{1,0:T(8,128)(2,1)} %copy-done.29, bf16[256,768]{1,0:T(8,128)(2,1)} %copy-done.18, bf16[768,3072]{1,0:T(8,128)(2,1)} %bitcast.40, ...), custom_call_target="tpu_custom_call" | custom-call | flops 1 | bytes 1 | tf_op jit(solution)/shard_map/expert/pallas_call | solution.py:74
  111.3 10.2 %expert.7 = (bf16[3072,256]{1,0:T(8,128)(2,1)}, bf16[256,3072]{1,0:T(8,128)(2,1)}, bf16[256,768]{1,0:T(8,128)(2,1)}, bf16[256,768]{1,0:T(8,128)(2,1)}, bf16[768,256]{1,0:T(8,128)(2,1)}) custom-call(bf16[256,768]{1,0:T(8,128)(2,1)} %copy-done.28, bf16[256,768]{1,0:T(8,128)(2,1)} %copy-done.19, bf16[768,3072]{1,0:T(8,128)(2,1)} %bitcast.41, ...), custom_call_target="tpu_custom_call" | custom-call | flops 1 | bytes 1 | tf_op jit(solution)/shard_map/expert/pallas_call | solution.py:74
  124.6 16.3 %expert_grad.1 = (bf16[1536,768]{1,0:T(8,128)(2,1)}, bf16[1536,768]{1,0:T(8,128)(2,1)}, bf16[1536,768]{1,0:T(8,128)(2,1)}, bf16[1536,768]{1,0:T(8,128)(2,1)}) custom-call(s32[5]{0:T(128)} %stack.52.chip_ref.meta_ref, bf16[768,256]{1,0:T(8,128)(2,1)} %get-tuple-element.201.refs_0_, bf16[768,256]{1,0:T(8,128)(2,1)} %get-tuple-element.202.refs_1_, ...), custom_call_target="tpu_custom_call" | custom-call | flops 1 | bytes 1 | tf_op jit(solution)/shard_map/expert_grad/pallas_call | solution.py:74
  141.7 5.2 %lower.1 = (f32[512,768]{1,0:T(8,128)}, bf16[512,768]{1,0:T(8,128)(2,1)}, f32[1,768]{1,0:T(1,128)}, f32[1,768]{1,0:T(1,128)}) custom-call(s32[512,1]{1,0:T(8,128)} %get-tuple-element.165.slot_ref, f32[512,768]{1,0:T(8,128)} %get-tuple-element.184.resid_ref, bf16[512,768]{1,0:T(8,128)(2,1)} %bitcast.57, f32[24,128]{1,0:T(8,128)} %pad_maximum_fusion.5.norm_ref, ...), custom_call_target="tpu_custom_call" | custom-call | flops 1 | bytes 1 | tf_op jit(solution)/shard_map/lower/pallas_call | solution.py:74
  163.6 22.0 %attend_back.1 = (bf16[1024,384]{1,0:T(8,128)(2,1)}, bf16[2048,384]{1,0:T(8,128)(2,1)}, bf16[2048,384]{1,0:T(8,128)(2,1)}) custom-call(s32[1,128]{1,0:T(1,128)} %get-tuple-element.173.meta_ref, bf16[1024,384]{1,0:T(8,128)(2,1)} %get-tuple-element.167.q_ref.q_hbm, bf16[2048,384]{1,0:T(8,128)(2,1)} %get-tuple-element.174.k_ref.k_hbm, ...), custom_call_target="tpu_custom_call" | custom-call | flops 1 | bytes 1 | tf_op jit(solution)/shard_map/attend_back/pallas_call | solution.py:74
  185.6 10.0 %dense.1 = (bf16[2304,128]{1,0:T(8,128)(2,1)}, bf16[2304,128]{1,0:T(8,128)(2,1)}, bf16[2304,128]{1,0:T(8,128)(2,1)}, bf16[2304,128]{1,0:T(8,128)(2,1)}) custom-call(s32[5]{0:T(128)} %stack.52.chip_ref.meta_ref, bf16[2048,768]{1,0:T(8,128)(2,1)} %get-tuple-element.172.a_hbm, bf16[1024,384]{1,0:T(8,128)(2,1)} %get-tuple-element.254.gq_hbm.gq_ref, ...), custom_call_target="tpu_custom_call" | custom-call | flops 1 | bytes 1 | tf_op jit(solution)/shard_map/dense/pallas_call | solution.py:74
  195.6 6.3 %collective-permute-start.19 = (bf16[2304,128]{1,0:T(8,128)(2,1)}, bf16[2304,128]{1,0:T(8,128)(2,1)}, u32[]{:S(2)}, u32[]{:S(2)}) collective-permute-start(bf16[2304,128]{1,0:T(8,128)(2,1)} %get-tuple-element.248), channel_id=1, source_target_pairs={{0,8},{4,12},{8,0},{12,4},{16,24},{20,28},{24,16},{28,20},{1,9},{5... | collective-permute-start | bytes 1769480 | tf_op jit(solution)/shard_map/ppermute | solution.py:889
  207.7 13.3 %project_back.1 = (f32[512,768]{1,0:T(8,128)}, bf16[1024,768]{1,0:T(8,128)(2,1)}, f32[512,768]{1,0:T(8,128)}, f32[1,768]{1,0:T(1,128)}, f32[1,768]{1,0:T(1,128)}) custom-call(s32[1]{0:T(128)} %bitcast.core_ref, bf16[512,768]{1,0:T(8,128)(2,1)} %bitcast.50, bf16[512,768]{1,0:T(8,128)(2,1)} %copy-done.5, bf16[512,768]{1,0:T(8,128)(2,1)} %copy-done.3, ...), custom_call_target="tpu_custom_call" | custom-call | flops 1 | bytes 1 | tf_op jit(solution)/shard_map/project_back/pallas_call | solution.py:74
  221.0 6.3 %collective-permute-done.24 = bf16[384,768]{1,0:T(8,128)(2,1)S(1)} collective-permute-done((bf16[384,768]{1,0:T(8,128)(2,1)S(1)}, bf16[384,768]{1,0:T(8,128)(2,1)S(1)}, u32[]{:S(2)}, u32[]{:S(2)}) %collective-permute-start.24) | collective-permute-done | bytes 589856 | tf_op jit(solution)/shard_map/ppermute | solution.py:889
  235.1 4.8 %collective-permute-done.26 = bf16[1152,128]{1,0:T(8,128)(2,1)S(1)} collective-permute-done((bf16[1152,128]{1,0:T(8,128)(2,1)S(1)}, bf16[1152,128]{1,0:T(8,128)(2,1)S(1)}, u32[]{:S(2)}, u32[]{:S(2)}) %collective-permute-start.26) | collective-permute-done | bytes 294944 | tf_op jit(solution)/shard_map/ppermute | solution.py:889
  253.8 8.7 %collective-permute-done.28 = bf16[384,768]{1,0:T(8,128)(2,1)} collective-permute-done((bf16[384,768]{1,0:T(8,128)(2,1)S(1)}, bf16[384,768]{1,0:T(8,128)(2,1)}, u32[]{:S(2)}, u32[]{:S(2)}) %collective-permute-start.28) | collective-permute-done | bytes 589856 | tf_op jit(solution)/shard_map/ppermute | solution.py:889
  268.9 4.8 %all-to-all-start.1 = ((bf16[4,2,288,128]{3,2,1,0:T(8,128)(2,1)}), bf16[4,2,288,128]{3,2,1,0:T(8,128)(2,1)S(1)}, u32[]{:S(2)}, u32[]{:S(2)}) async-start(bf16[4,2,288,128]{3,2,1,0:T(8,128)(2,1)} %broadcast_in_dim.16), calls=%async_computation.1 | async-start | bytes 1179648 | tf_op jit(solution)/shard_map/all_to_all | solution.py:893
  275.6 19.5 %collective-permute-done.36 = f32[4,768]{1,0:T(4,128)S(1)} collective-permute-done((f32[4,768]{1,0:T(4,128)S(1)}, f32[4,768]{1,0:T(4,128)S(1)}, u32[]{:S(2)}, u32[]{:S(2)}) %collective-permute-start.36) | collective-permute-done | bytes 12320 | tf_op jit(solution)/shard_map/ppermute | solution.py:889
  299.9 7.5 %widen.2 = (f32[768,3072]{1,0:T(8,128)}, f32[3072,768]{1,0:T(8,128)}) custom-call(s32[5]{0:T(128)} %stack.52.chip_ref.meta_ref, bf16[768,768]{1,0:T(8,128)(2,1)} %copy-done.2, bf16[768,768]{1,0:T(8,128)(2,1)} %collective-permute-done.32.refs_1_, bf16[768,768]{1,0:T(8,128)(2,1)} %copy-done.1, bf16[768,768]{1,0:T(8,128)(2,1)} %collective-permute-done.33.refs_3_), custom_call_target="tpu_custom_call" | custom-call | flops 1 | bytes 1 | tf_op jit(solution)/shard_map/widen/pallas_call | solution.py:74
  316.8 7.6 %widen.3 = (f32[768,3072]{1,0:T(8,128)}, f32[3072,768]{1,0:T(8,128)}) custom-call(s32[5]{0:T(128)} %stack.58.meta_ref, bf16[768,768]{1,0:T(8,128)(2,1)} %collective-permute-done.34.refs_0_, bf16[768,768]{1,0:T(8,128)(2,1)} %copy-done.21, bf16[768,768]{1,0:T(8,128)(2,1)} %collective-permute-done.35.refs_2_, ...), custom_call_target="tpu_custom_call", output_to_operand_aliasing={{0}: (5, {}), {1}: (6, {})} | custom-call | flops 1 | bytes 1 | tf_op jit(solution)/shard_map/widen/pallas_call | solution.py:74
  336.2 6.8 %spread_columns.1 = f32[768,2304]{1,0:T(8,128)} custom-call(s32[5]{0:T(128)} %stack.52.chip_ref.meta_ref, bf16[2,3,384,128]{3,2,1,0:T(8,128)(2,1)} %bitcast.64, bf16[2,3,384,128]{3,2,1,0:T(8,128)(2,1)} %bitcast.25.refs_1_, bf16[2,3,384,128]{3,2,1,0:T(8,128)(2,1)} %bitcast.55, bf16[2,3,384,128]{3,2,1,0:T(8,128)(2,1)} %bitcast.59, ...), custom_call_target="tpu_custom_call" | custom-call | flops 1 | bytes 1 | tf_op jit(solution)/shard_map/spread_columns/pallas_call | solution.py:74
  (226 shorter events, 116.9 us)
Async XLA Ops:
  1.2 22.2 %collective-permute-start = (bf16[512,768]{1,0:T(8,128)(2,1)}, bf16[512,768]{1,0:T(8,128)(2,1)S(1)}, u32[]{:S(2)}, u32[]{:S(2)}) collective-permute-start(bf16[512,768]{1,0:T(8,128)(2,1)} %bitcast.47), channel_id=1, source_target_pairs={{0,8},{4,12},{8,16},{12,20},{16,24},{20,28},{1,9},{5,13},{9,17},{1... | collective-permute-start | bytes 2359304 | tf_op jit(solution)/shard_map/ppermute | solution.py:899
  23.3 30.8 %collective-permute-start.4 = (bf16[256,768]{1,0:T(8,128)(2,1)S(1)}, bf16[256,768]{1,0:T(8,128)(2,1)S(1)}, u32[]{:S(2)}, u32[]{:S(2)}) collective-permute-start(bf16[256,768]{1,0:T(8,128)(2,1)S(1)} %copy-done.47), channel_id=1, source_target_pairs={{0,1},{1,0},{2,3},{3,2},{4,5},{5,4},{6,7},{7,6},{8,9},{9,8},{10,11... | collective-permute-start | bytes 1179656 | tf_op jit(solution)/shard_map/ppermute | solution.py:889
  24.9 29.7 %collective-permute-start.5 = (bf16[256,768]{1,0:T(8,128)(2,1)S(1)}, bf16[256,768]{1,0:T(8,128)(2,1)S(1)}, u32[]{:S(2)}, u32[]{:S(2)}) collective-permute-start(bf16[256,768]{1,0:T(8,128)(2,1)S(1)} %copy-done.46), channel_id=1, source_target_pairs={{0,2},{1,3},{2,0},{3,1},{4,6},{5,7},{6,4},{7,5},{8,10},{9,11},{10,... | collective-permute-start | bytes 1179656 | tf_op jit(solution)/shard_map/ppermute | solution.py:889
  27.5 27.2 %collective-permute-start.6 = (bf16[256,768]{1,0:T(8,128)(2,1)S(1)}, bf16[256,768]{1,0:T(8,128)(2,1)S(1)}, u32[]{:S(2)}, u32[]{:S(2)}) collective-permute-start(bf16[256,768]{1,0:T(8,128)(2,1)S(1)} %copy-done.45), channel_id=1, source_target_pairs={{0,3},{1,2},{2,1},{3,0},{4,7},{5,6},{6,5},{7,4},{8,11},{9,10},{10,... | collective-permute-start | bytes 1179656 | tf_op jit(solution)/shard_map/ppermute | solution.py:889
  62.6 23.3 %collective-permute-start.7 = (bf16[256,768]{1,0:T(8,128)(2,1)}, bf16[256,768]{1,0:T(8,128)(2,1)S(1)}, u32[]{:S(2)}, u32[]{:S(2)}) collective-permute-start(bf16[256,768]{1,0:T(8,128)(2,1)} %get-tuple-element.187), channel_id=1, source_target_pairs={{0,1},{1,0},{2,3},{3,2},{4,5},{5,4},{6,7},{7,6},{8,9},{9,8},{10,11... | collective-permute-start | bytes 1179656 | tf_op jit(solution)/shard_map/ppermute | solution.py:889
  69.5 30.0 %collective-permute-start.8 = (bf16[256,768]{1,0:T(8,128)(2,1)}, bf16[256,768]{1,0:T(8,128)(2,1)S(1)}, u32[]{:S(2)}, u32[]{:S(2)}) collective-permute-start(bf16[256,768]{1,0:T(8,128)(2,1)} %get-tuple-element.191), channel_id=1, source_target_pairs={{0,2},{1,3},{2,0},{3,1},{4,6},{5,7},{6,4},{7,5},{8,10},{9,11},{10,... | collective-permute-start | bytes 1179656 | tf_op jit(solution)/shard_map/ppermute | solution.py:889
  70.5 40.0 %collective-permute-start.9 = (bf16[256,768]{1,0:T(8,128)(2,1)}, bf16[256,768]{1,0:T(8,128)(2,1)S(1)}, u32[]{:S(2)}, u32[]{:S(2)}) collective-permute-start(bf16[256,768]{1,0:T(8,128)(2,1)} %get-tuple-element.195), channel_id=1, source_target_pairs={{0,3},{1,2},{2,1},{3,0},{4,7},{5,6},{6,5},{7,4},{8,11},{9,10},{10,... | collective-permute-start | bytes 1179656 | tf_op jit(solution)/shard_map/ppermute | solution.py:889
  96.7 27.9 %collective-permute-start.10 = (bf16[256,768]{1,0:T(8,128)(2,1)}, bf16[256,768]{1,0:T(8,128)(2,1)S(1)}, u32[]{:S(2)}, u32[]{:S(2)}) collective-permute-start(bf16[256,768]{1,0:T(8,128)(2,1)} %get-tuple-element.192), channel_id=1, source_target_pairs={{0,1},{1,0},{2,3},{3,2},{4,5},{5,4},{6,7},{7,6},{8,9},{9,8},{10,11... | collective-permute-start | bytes 1179656 | tf_op jit(solution)/shard_map/ppermute | solution.py:889
  110.4 30.4 %collective-permute-start.11 = (bf16[256,768]{1,0:T(8,128)(2,1)}, bf16[256,768]{1,0:T(8,128)(2,1)S(1)}, u32[]{:S(2)}, u32[]{:S(2)}) collective-permute-start(bf16[256,768]{1,0:T(8,128)(2,1)} %get-tuple-element.196), channel_id=1, source_target_pairs={{0,2},{1,3},{2,0},{3,1},{4,6},{5,7},{6,4},{7,5},{8,10},{9,11},{10,... | collective-permute-start | bytes 1179656 | tf_op jit(solution)/shard_map/ppermute | solution.py:889
  152.6 49.4 %collective-permute-start.22 = (bf16[768,768]{1,0:T(8,128)(2,1)S(1)}, bf16[768,768]{1,0:T(8,128)(2,1)}, u32[]{:S(2)}, u32[]{:S(2)}) collective-permute-start(bf16[768,768]{1,0:T(8,128)(2,1)S(1)} %add_convert_fusion), channel_id=1, source_target_pairs={{0,16},{4,20},{8,24},{12,28},{16,0},{20,4},{24,8},{28,12},{1,17},{... | collective-permute-start | bytes 3538952 | tf_op jit(solution)/shard_map/ppermute | solution.py:889
  157.3 44.7 %collective-permute-start.21 = (bf16[768,768]{1,0:T(8,128)(2,1)}, bf16[768,768]{1,0:T(8,128)(2,1)}, u32[]{:S(2)}, u32[]{:S(2)}) collective-permute-start(bf16[768,768]{1,0:T(8,128)(2,1)} %add_convert_fusion.1), channel_id=1, source_target_pairs={{0,8},{4,12},{8,0},{12,4},{16,24},{20,28},{24,16},{28,20},{1,9},{5... | collective-permute-start | bytes 3538952 | tf_op jit(solution)/shard_map/ppermute | solution.py:889
  157.9 37.7 %collective-permute-start.16 = (bf16[256,768]{1,0:T(8,128)(2,1)}, bf16[256,768]{1,0:T(8,128)(2,1)}, u32[]{:S(2)}, u32[]{:S(2)}) collective-permute-start(bf16[256,768]{1,0:T(8,128)(2,1)} %get-tuple-element.244), channel_id=1, source_target_pairs={{0,1},{1,0},{2,3},{3,2},{4,5},{5,4},{6,7},{7,6},{8,9},{9,8},{10,11... | collective-permute-start | bytes 1179656 | tf_op jit(solution)/shard_map/ppermute | solution.py:889
  161.2 34.4 %collective-permute-start.17 = (bf16[256,768]{1,0:T(8,128)(2,1)}, bf16[256,768]{1,0:T(8,128)(2,1)}, u32[]{:S(2)}, u32[]{:S(2)}) collective-permute-start(bf16[256,768]{1,0:T(8,128)(2,1)} %get-tuple-element.245), channel_id=1, source_target_pairs={{0,2},{1,3},{2,0},{3,1},{4,6},{5,7},{6,4},{7,5},{8,10},{9,11},{10,... | collective-permute-start | bytes 1179656 | tf_op jit(solution)/shard_map/ppermute | solution.py:889
  161.7 34.0 %collective-permute-start.18 = (bf16[256,768]{1,0:T(8,128)(2,1)}, bf16[256,768]{1,0:T(8,128)(2,1)}, u32[]{:S(2)}, u32[]{:S(2)}) collective-permute-start(bf16[256,768]{1,0:T(8,128)(2,1)} %get-tuple-element.246), channel_id=1, source_target_pairs={{0,3},{1,2},{2,1},{3,0},{4,7},{5,6},{6,5},{7,4},{8,11},{9,10},{10,... | collective-permute-start | bytes 1179656 | tf_op jit(solution)/shard_map/ppermute | solution.py:889
  195.6 25.4 %collective-permute-start.19 = (bf16[2304,128]{1,0:T(8,128)(2,1)}, bf16[2304,128]{1,0:T(8,128)(2,1)}, u32[]{:S(2)}, u32[]{:S(2)}) collective-permute-start(bf16[2304,128]{1,0:T(8,128)(2,1)} %get-tuple-element.248), channel_id=1, source_target_pairs={{0,8},{4,12},{8,0},{12,4},{16,24},{20,28},{24,16},{28,20},{1,9},{5... | collective-permute-start | bytes 1769480 | tf_op jit(solution)/shard_map/ppermute | solution.py:889
  203.4 23.9 %collective-permute-start.24 = (bf16[384,768]{1,0:T(8,128)(2,1)S(1)}, bf16[384,768]{1,0:T(8,128)(2,1)S(1)}, u32[]{:S(2)}, u32[]{:S(2)}) collective-permute-start(bf16[384,768]{1,0:T(8,128)(2,1)S(1)} %add_convert_fusion.7), channel_id=1, source_target_pairs={{0,8},{4,12},{8,0},{12,4},{16,24},{20,28},{24,16},{28,20},{1,9},{5... | collective-permute-start | bytes 1769480 | tf_op jit(solution)/shard_map/ppermute | solution.py:889
  205.7 23.1 %collective-permute-start.23 = (bf16[384,768]{1,0:T(8,128)(2,1)}, bf16[384,768]{1,0:T(8,128)(2,1)S(1)}, u32[]{:S(2)}, u32[]{:S(2)}) collective-permute-start(bf16[384,768]{1,0:T(8,128)(2,1)} %add_convert_fusion.8), channel_id=1, source_target_pairs={{0,16},{4,20},{8,24},{12,28},{16,0},{20,4},{24,8},{28,12},{1,17},{... | collective-permute-start | bytes 1769480 | tf_op jit(solution)/shard_map/ppermute | solution.py:889
  266.3 28.8 %collective-permute-start.34 = (bf16[768,768]{1,0:T(8,128)(2,1)S(1)}, bf16[768,768]{1,0:T(8,128)(2,1)}, u32[]{:S(2)}, u32[]{:S(2)}) collective-permute-start(bf16[768,768]{1,0:T(8,128)(2,1)S(1)} %pad_maximum_fusion.refs_0_), channel_id=1, source_target_pairs={{0,4},{4,0},{8,12},{12,8},{16,20},{20,16},{24,28},{28,24},{1,5},{5... | collective-permute-start | bytes 3538952 | tf_op jit(solution)/shard_map/ppermute | solution.py:889
  266.4 28.7 %collective-permute-start.35 = (bf16[768,768]{1,0:T(8,128)(2,1)S(1)}, bf16[768,768]{1,0:T(8,128)(2,1)}, u32[]{:S(2)}, u32[]{:S(2)}) collective-permute-start(bf16[768,768]{1,0:T(8,128)(2,1)S(1)} %pad_maximum_fusion.1.refs_2_), channel_id=1, source_target_pairs={{0,4},{4,0},{8,12},{12,8},{16,20},{20,16},{24,28},{28,24},{1,5},{5... | collective-permute-start | bytes 3538952 | tf_op jit(solution)/shard_map/ppermute | solution.py:889
  266.9 28.2 %collective-permute-start.33 = (bf16[768,768]{1,0:T(8,128)(2,1)S(1)}, bf16[768,768]{1,0:T(8,128)(2,1)}, u32[]{:S(2)}, u32[]{:S(2)}) collective-permute-start(bf16[768,768]{1,0:T(8,128)(2,1)S(1)} %pad_maximum_fusion.1.refs_2_), channel_id=1, source_target_pairs={{0,16},{4,20},{8,24},{12,28},{16,0},{20,4},{24,8},{28,12},{1,17},{... | collective-permute-start | bytes 3538952 | tf_op jit(solution)/shard_map/ppermute | solution.py:889
  267.2 28.0 %collective-permute-start.32 = (bf16[768,768]{1,0:T(8,128)(2,1)S(1)}, bf16[768,768]{1,0:T(8,128)(2,1)}, u32[]{:S(2)}, u32[]{:S(2)}) collective-permute-start(bf16[768,768]{1,0:T(8,128)(2,1)S(1)} %pad_maximum_fusion.refs_0_), channel_id=1, source_target_pairs={{0,8},{4,12},{8,0},{12,4},{16,24},{20,28},{24,16},{28,20},{1,9},{5... | collective-permute-start | bytes 3538952 | tf_op jit(solution)/shard_map/ppermute | solution.py:889
  268.9 26.2 %all-to-all-start.1 = ((bf16[4,2,288,128]{3,2,1,0:T(8,128)(2,1)}), bf16[4,2,288,128]{3,2,1,0:T(8,128)(2,1)S(1)}, u32[]{:S(2)}, u32[]{:S(2)}) async-start(bf16[4,2,288,128]{3,2,1,0:T(8,128)(2,1)} %broadcast_in_dim.16), calls=%async_computation.1 | async-start | bytes 1179648 | tf_op jit(solution)/shard_map/all_to_all | solution.py:893
  273.8 21.3 %collective-permute-start.36 = (f32[4,768]{1,0:T(4,128)S(1)}, f32[4,768]{1,0:T(4,128)S(1)}, u32[]{:S(2)}, u32[]{:S(2)}) collective-permute-start(f32[4,768]{1,0:T(4,128)S(1)} %fusion), channel_id=1, source_target_pairs={{0,16},{4,20},{8,24},{12,28},{16,0},{20,4},{24,8},{28,12},{1,17},{... | collective-permute-start | bytes 36872 | tf_op jit(solution)/shard_map/ppermute | solution.py:889
  314.9 28.6 %collective-permute-start.31 = (bf16[512,768]{1,0:T(8,128)(2,1)}, bf16[512,768]{1,0:T(8,128)(2,1)S(1)}, u32[]{:S(2)}, u32[]{:S(2)}) collective-permute-start(bf16[512,768]{1,0:T(8,128)(2,1)} %add_convert_fusion.2), channel_id=1, source_target_pairs={{8,0},{12,4},{16,8},{20,12},{24,16},{28,20},{9,1},{13,5},{17,9},{2... | collective-permute-start | bytes 2359304 | tf_op jit(solution)/shard_map/ppermute | solution.py:899
  (76 other events, 732.1 us)
where the time goes:
time: 350 us; the launch traced here: 349 us
  Pallas kernels  185 us (53%)
  starting transfers between devices  68.7 us (20%)
  waiting for transfers between devices  56.5 us (16%)
  other arithmetic  22.6 us (6%)
  local copies, waits for them, and re-layouts  14.6 us (4%)
    pallas_call x20, Pallas kernels, call(): pl.pallas_call(body, name=name, out_shape=out_shape, grid_spec=pltpu.Pref...  185 us
    ppermute x48, waiting for transfers between devices, swap(): lax.ppermute(block, axis, [(i, i ^ distance) for i in range(lax.axis_size...  55.6 us
    ppermute x48, starting transfers between devices, swap(): lax.ppermute(block, axis, [(i, i ^ distance) for i in range(lax.axis_size...  54.7 us
    convert_element_type x10, other arithmetic, total(): return sum((t.astype(F32) for t in terms)).astype(BF16)  16.1 us
    unnamed x96, local copies, waits for them, and re-layouts  10.4 us
    all_to_all x2, starting transfers between devices, trade(): return lax.all_to_all(block, axis, split_axis=0, concat_axis=0, tiled=True)  8.25 us
  transfers between devices with their start and end apart: 52, of which 14 were waited for; matrix products, arithmetic and copies ran while one was open for 7% of the time, Pallas kernels for 50%

commit v1 on v0

--- a/solution.py
+++ b/solution.py
@@ -390,7 +390,7 @@
                 grads_ref[2 * g + h, here, :] = part
         return unused
 
-    lax.fori_loop(0, total // TILE, begin, 0)
+    lax.fori_loop(0, total // TILE, begin, 0, unroll=2)
     waits[4]()
     put_heads(heads_ref, q_ref)
     waits[5]()
@@ -400,7 +400,7 @@
         kt_ref[:, here] = flip(k_ref[here, :])
         return unused
 
-    lax.fori_loop(0, 2 * total // TILE, turn, 0)
+    lax.fori_loop(0, 2 * total // TILE, turn, 0, unroll=2)
     waits[6]()
 
     def tile(t, unused):
@@ -1165,12 +1165,13 @@
     (near,) = meet([dense], (near,))
     for rest in range(len(bits) - 2):
         meet([dense, experts])
-    far = shift(add(halo, near[local_len:]), "seq", -2)
+    far = add(halo, near[local_len:])
     hops = [("seq", bit) for bit in bits + [1]]
     hops += [("exp", 1 << b) for b in range(sources.bit_length() - 1)]
     small = Stream(small_steps(small, hops))
     layer_output = finish(slot, resid, returned)
-    (layer_output,) = meet([dense, experts, small], (layer_output,))
+    layer_output, far = meet([dense, experts, small], (layer_output, far))
+    far = shift(far, "seq", -2)
     for rest in range(len(bits) - 2):
         meet([experts])
     own_parts = experts.result

time: 350 us -> 348 us (level)
    unnamed x96 -> x92, local copies, waits for them, and re-layouts: 10.4 us -> 9.87 us
  transfers between devices with their start and end apart: 52 -> 52, of which waited for: 14 -> 16; matrix products, arithmetic and copies ran while one was open for 7% -> 6% of each run, Pallas kernels for 50% -> 50%
where the time goes in v1:
time: 348 us; the launch traced here: 346 us
  Pallas kernels  184 us (53%)
  starting transfers between devices  71.7 us (21%)
  waiting for transfers between devices  55.3 us (16%)
  other arithmetic  20.1 us (6%)
  local copies, waits for them, and re-layouts  14 us (4%)
    pallas_call x20, Pallas kernels, call(): pl.pallas_call(body, name=name, out_shape=out_shape, grid_spec=pltpu.Pref...  184 us
    ppermute x48, waiting for transfers between devices, swap(): lax.ppermute(block, axis, [(i, i ^ distance) for i in range(lax.axis_size...  54.4 us
    ppermute x48, starting transfers between devices, swap(): lax.ppermute(block, axis, [(i, i ^ distance) for i in range(lax.axis_size...  54.3 us
    convert_element_type x10, other arithmetic, total(): return sum((t.astype(F32) for t in terms)).astype(BF16)  12.7 us
    all_to_all x2, starting transfers between devices, trade(): return lax.all_to_all(block, axis, split_axis=0, concat_axis=0, tiled=True)  11.7 us
    unnamed x92, local copies, waits for them, and re-layouts  9.87 us
  transfers between devices with their start and end apart: 52, of which 16 were waited for; matrix products, arithmetic and copies ran while one was open for 6% of the time, Pallas kernels for 50%

profile of v1, /device:TPU:0, one launch (start us, length us, event | category | flops | bytes accessed | tf_op | source)
XLA Modules:
  0.0 346.3 jit_solution(10090291124780126997)
XLA Ops:
  1.2 4.5 %collective-permute-start = (bf16[512,768]{1,0:T(8,128)(2,1)}, bf16[512,768]{1,0:T(8,128)(2,1)S(1)}, u32[]{:S(2)}, u32[]{:S(2)}) collective-permute-start(bf16[512,768]{1,0:T(8,128)(2,1)} %bitcast.47), channel_id=1, source_target_pairs={{0,8},{4,12},{8,16},{12,20},{16,24},{20,28},{1,9},{5,13},{9,17},{1... | collective-permute-start | bytes 2359304 | tf_op jit(solution)/shard_map/ppermute | solution.py:899
  7.6 5.0 %route.1 = (s32[512,1]{1,0:T(8,128)}, s32[1,1024]{1,0:T(1,128)}, s32[1024,1]{1,0:T(8,128)}, s32[1,128]{1,0:T(1,128)}, bf16[256,768]{1,0:T(8,128)(2,1)}, /*index=...) custom-call(s32[3]{0:T(128)} %pad_add_fusion.at_ref, s32[1,512]{1,0:T(1,128)} %ids_ref.1, ...), custom_call_target="tpu_custom_call" | custom-call | flops 1 | bytes 1 | tf_op jit(solution)/shard_map/route/pallas_call | solution.py:74
  14.8 7.6 %project.2 = (bf16[2048,768]{1,0:T(8,128)(2,1)}, bf16[2048,384]{1,0:T(8,128)(2,1)}, bf16[2048,384]{1,0:T(8,128)(2,1)}, bf16[1024,384]{1,0:T(8,128)(2,1)}) custom-call(s32[1]{0:T(128)} %bitcast.core_ref, bf16[512,768]{1,0:T(8,128)(2,1)} %bitcast.48, bf16[512,768]{1,0:T(8,128)(2,1)} %copy-done.6, f32[24,128]{1,0:T(8,128)} %pad_maximum_fusion.5.norm_ref, ...), custom_call_target="tpu_custom_call" | custom-call | flops 1 | bytes 1 | tf_op jit(solution)/shard_map/project/pallas_call | solution.py:74
  28.6 6.5 %project.3 = (bf16[2048,768]{1,0:T(8,128)(2,1)}, bf16[2048,384]{1,0:T(8,128)(2,1)}, bf16[2048,384]{1,0:T(8,128)(2,1)}) custom-call(s32[1]{0:T(128)} %bitcast.core_ref, bf16[512,768]{1,0:T(8,128)(2,1)} %copy-done.4, bf16[512,768]{1,0:T(8,128)(2,1)} %copy-done.5, ...), custom_call_target="tpu_custom_call", output_to_operand_aliasing={{0}: (7, {}), {1}: (8, {}), {2}: (9, {})} | custom-call | flops 1 | bytes 1 | tf_op jit(solution)/shard_map/project/pallas_call | solution.py:74
  35.1 19.0 %attend.1 = (bf16[512,384]{1,0:T(8,128)(2,1)}, bf16[512,384]{1,0:T(8,128)(2,1)}, bf16[1024,384]{1,0:T(8,128)(2,1)}, f32[384,1024]{1,0:T(8,128)}, f32[8,1024]{1,0:T(8,128)}) custom-call(s32[1,128]{1,0:T(1,128)} %get-tuple-element.174.meta_ref, bf16[1024,384]{1,0:T(8,128)(2,1)} %get-tuple-element.168.q_ref.q_hbm, ...), custom_call_target="tpu_custom_call" | custom-call | flops 1 | bytes 1 | tf_op jit(solution)/shard_map/attend/pallas_call | solution.py:74
  56.8 5.8 %lift.1 = (f32[512,768]{1,0:T(8,128)}, bf16[256,768]{1,0:T(8,128)(2,1)}, bf16[256,768]{1,0:T(8,128)(2,1)}, bf16[256,768]{1,0:T(8,128)(2,1)}, bf16[256,768]{1,0:T(8,128)(2,1)}) custom-call(s32[1]{0:T(128)} %bitcast.core_ref, bf16[512,384]{1,0:T(8,128)(2,1)} %get-tuple-element.178.own_ref, bf16[512,384]{1,0:T(8,128)(2,1)} %copy-done.35, ...), custom_call_target="tpu_custom_call" | custom-call | flops 1 | bytes 1 | tf_op jit(solution)/shard_map/lift/pallas_call | solution.py:74
  62.6 6.9 %collective-permute-start.7 = (bf16[256,768]{1,0:T(8,128)(2,1)}, bf16[256,768]{1,0:T(8,128)(2,1)S(1)}, u32[]{:S(2)}, u32[]{:S(2)}) collective-permute-start(bf16[256,768]{1,0:T(8,128)(2,1)} %get-tuple-element.188), channel_id=1, source_target_pairs={{0,1},{1,0},{2,3},{3,2},{4,5},{5,4},{6,7},{7,6},{8,9},{9,8},{10,11... | collective-permute-start | bytes 1179656 | tf_op jit(solution)/shard_map/ppermute | solution.py:889
  72.0 10.1 %expert.4 = (bf16[3072,256]{1,0:T(8,128)(2,1)}, bf16[256,3072]{1,0:T(8,128)(2,1)}, bf16[256,768]{1,0:T(8,128)(2,1)}, bf16[256,768]{1,0:T(8,128)(2,1)}, bf16[768,256]{1,0:T(8,128)(2,1)}) custom-call(bf16[256,768]{1,0:T(8,128)(2,1)} %get-tuple-element.186.rows_ref, bf16[256,768]{1,0:T(8,128)(2,1)} %get-tuple-element.180.grad_ref.refs_4_, ...), custom_call_target="tpu_custom_call" | custom-call | flops 1 | bytes 1 | tf_op jit(solution)/shard_map/expert/pallas_call | solution.py:74
  86.6 10.1 %expert.5 = (bf16[3072,256]{1,0:T(8,128)(2,1)}, bf16[256,3072]{1,0:T(8,128)(2,1)}, bf16[256,768]{1,0:T(8,128)(2,1)}, bf16[256,768]{1,0:T(8,128)(2,1)}, bf16[768,256]{1,0:T(8,128)(2,1)}) custom-call(bf16[256,768]{1,0:T(8,128)(2,1)} %copy-done.30, bf16[256,768]{1,0:T(8,128)(2,1)} %copy-done.16, bf16[768,3072]{1,0:T(8,128)(2,1)} %bitcast.39, ...), custom_call_target="tpu_custom_call" | custom-call | flops 1 | bytes 1 | tf_op jit(solution)/shard_map/expert/pallas_call | solution.py:74
  100.3 10.1 %expert.6 = (bf16[3072,256]{1,0:T(8,128)(2,1)}, bf16[256,3072]{1,0:T(8,128)(2,1)}, bf16[256,768]{1,0:T(8,128)(2,1)}, bf16[256,768]{1,0:T(8,128)(2,1)}, bf16[768,256]{1,0:T(8,128)(2,1)}) custom-call(bf16[256,768]{1,0:T(8,128)(2,1)} %copy-done.29, bf16[256,768]{1,0:T(8,128)(2,1)} %copy-done.17, bf16[768,3072]{1,0:T(8,128)(2,1)} %bitcast.40, ...), custom_call_target="tpu_custom_call" | custom-call | flops 1 | bytes 1 | tf_op jit(solution)/shard_map/expert/pallas_call | solution.py:74
  111.3 10.2 %expert.7 = (bf16[3072,256]{1,0:T(8,128)(2,1)}, bf16[256,3072]{1,0:T(8,128)(2,1)}, bf16[256,768]{1,0:T(8,128)(2,1)}, bf16[256,768]{1,0:T(8,128)(2,1)}, bf16[768,256]{1,0:T(8,128)(2,1)}) custom-call(bf16[256,768]{1,0:T(8,128)(2,1)} %copy-done.28, bf16[256,768]{1,0:T(8,128)(2,1)} %copy-done.18, bf16[768,3072]{1,0:T(8,128)(2,1)} %bitcast.41, ...), custom_call_target="tpu_custom_call" | custom-call | flops 1 | bytes 1 | tf_op jit(solution)/shard_map/expert/pallas_call | solution.py:74
  124.6 16.3 %expert_grad.1 = (bf16[1536,768]{1,0:T(8,128)(2,1)}, bf16[1536,768]{1,0:T(8,128)(2,1)}, bf16[1536,768]{1,0:T(8,128)(2,1)}, bf16[1536,768]{1,0:T(8,128)(2,1)}) custom-call(s32[5]{0:T(128)} %stack.52.chip_ref.meta_ref, bf16[768,256]{1,0:T(8,128)(2,1)} %get-tuple-element.202.refs_0_, bf16[768,256]{1,0:T(8,128)(2,1)} %get-tuple-element.203.refs_1_, ...), custom_call_target="tpu_custom_call" | custom-call | flops 1 | bytes 1 | tf_op jit(solution)/shard_map/expert_grad/pallas_call | solution.py:74
  141.8 5.3 %lower.1 = (f32[512,768]{1,0:T(8,128)}, bf16[512,768]{1,0:T(8,128)(2,1)}, f32[1,768]{1,0:T(1,128)}, f32[1,768]{1,0:T(1,128)}) custom-call(s32[512,1]{1,0:T(8,128)} %get-tuple-element.166.slot_ref, f32[512,768]{1,0:T(8,128)} %get-tuple-element.185.resid_ref, bf16[512,768]{1,0:T(8,128)(2,1)} %bitcast.57, f32[24,128]{1,0:T(8,128)} %pad_maximum_fusion.5.norm_ref, ...), custom_call_target="tpu_custom_call" | custom-call | flops 1 | bytes 1 | tf_op jit(solution)/shard_map/lower/pallas_call | solution.py:74
  165.7 20.9 %attend_back.1 = (bf16[1024,384]{1,0:T(8,128)(2,1)}, bf16[2048,384]{1,0:T(8,128)(2,1)}, bf16[2048,384]{1,0:T(8,128)(2,1)}) custom-call(s32[1,128]{1,0:T(1,128)} %get-tuple-element.174.meta_ref, bf16[1024,384]{1,0:T(8,128)(2,1)} %get-tuple-element.168.q_ref.q_hbm, bf16[2048,384]{1,0:T(8,128)(2,1)} %get-tuple-element.175.k_ref.k_hbm, ...), custom_call_target="tpu_custom_call" | custom-call | flops 1 | bytes 1 | tf_op jit(solution)/shard_map/attend_back/pallas_call | solution.py:74
  186.6 10.1 %dense.1 = (bf16[2304,128]{1,0:T(8,128)(2,1)}, bf16[2304,128]{1,0:T(8,128)(2,1)}, bf16[2304,128]{1,0:T(8,128)(2,1)}, bf16[2304,128]{1,0:T(8,128)(2,1)}) custom-call(s32[5]{0:T(128)} %stack.52.chip_ref.meta_ref, bf16[2048,768]{1,0:T(8,128)(2,1)} %get-tuple-element.173.a_hbm, bf16[1024,384]{1,0:T(8,128)(2,1)} %get-tuple-element.255.gq_hbm.gq_ref, ...), custom_call_target="tpu_custom_call" | custom-call | flops 1 | bytes 1 | tf_op jit(solution)/shard_map/dense/pallas_call | solution.py:74
  205.2 13.1 %project_back.1 = (f32[512,768]{1,0:T(8,128)}, bf16[1024,768]{1,0:T(8,128)(2,1)}, f32[512,768]{1,0:T(8,128)}, f32[1,768]{1,0:T(1,128)}, f32[1,768]{1,0:T(1,128)}) custom-call(s32[1]{0:T(128)} %bitcast.core_ref, bf16[512,768]{1,0:T(8,128)(2,1)} %bitcast.50, bf16[512,768]{1,0:T(8,128)(2,1)} %copy-done.6, bf16[512,768]{1,0:T(8,128)(2,1)} %copy-done.4, ...), custom_call_target="tpu_custom_call" | custom-call | flops 1 | bytes 1 | tf_op jit(solution)/shard_map/project_back/pallas_call | solution.py:74
  218.4 6.3 %collective-permute-done.24 = bf16[384,768]{1,0:T(8,128)(2,1)S(1)} collective-permute-done((bf16[384,768]{1,0:T(8,128)(2,1)}, bf16[384,768]{1,0:T(8,128)(2,1)S(1)}, u32[]{:S(2)}, u32[]{:S(2)}) %collective-permute-start.24) | collective-permute-done | bytes 589856 | tf_op jit(solution)/shard_map/ppermute | solution.py:889
  237.2 6.9 %all-to-all-start = ((bf16[4,2,288,128]{3,2,1,0:T(8,128)(2,1)}), bf16[4,2,288,128]{3,2,1,0:T(8,128)(2,1)S(1)}, u32[]{:S(2)}, u32[]{:S(2)}) async-start(bf16[4,2,288,128]{3,2,1,0:T(8,128)(2,1)} %pad_maximum_fusion.2), calls=%async_computation | async-start | bytes 1179648 | tf_op jit(solution)/shard_map/all_to_all | solution.py:893
  255.4 5.2 %collective-permute-done.28 = bf16[384,768]{1,0:T(8,128)(2,1)} collective-permute-done((bf16[384,768]{1,0:T(8,128)(2,1)S(1)}, bf16[384,768]{1,0:T(8,128)(2,1)}, u32[]{:S(2)}, u32[]{:S(2)}) %collective-permute-start.28) | collective-permute-done | bytes 589856 | tf_op jit(solution)/shard_map/ppermute | solution.py:889
  268.2 4.8 %all-to-all-start.1 = ((bf16[4,2,288,128]{3,2,1,0:T(8,128)(2,1)}), bf16[4,2,288,128]{3,2,1,0:T(8,128)(2,1)S(1)}, u32[]{:S(2)}, u32[]{:S(2)}) async-start(bf16[4,2,288,128]{3,2,1,0:T(8,128)(2,1)} %broadcast_in_dim.16), calls=%async_computation.1 | async-start | bytes 1179648 | tf_op jit(solution)/shard_map/all_to_all | solution.py:893
  274.1 19.0 %collective-permute-done.36 = f32[4,768]{1,0:T(4,128)S(1)} collective-permute-done((f32[4,768]{1,0:T(4,128)S(1)}, f32[4,768]{1,0:T(4,128)S(1)}, u32[]{:S(2)}, u32[]{:S(2)}) %collective-permute-start.36) | collective-permute-done | bytes 12320 | tf_op jit(solution)/shard_map/ppermute | solution.py:889
  298.3 7.5 %widen.2 = (f32[768,3072]{1,0:T(8,128)}, f32[3072,768]{1,0:T(8,128)}) custom-call(s32[5]{0:T(128)} %stack.52.chip_ref.meta_ref, bf16[768,768]{1,0:T(8,128)(2,1)} %copy-done.2, bf16[768,768]{1,0:T(8,128)(2,1)} %collective-permute-done.32.refs_1_, bf16[768,768]{1,0:T(8,128)(2,1)} %copy-done.1, bf16[768,768]{1,0:T(8,128)(2,1)} %collective-permute-done.33.refs_3_), custom_call_target="tpu_custom_call" | custom-call | flops 1 | bytes 1 | tf_op jit(solution)/shard_map/widen/pallas_call | solution.py:74
  315.3 7.6 %widen.3 = (f32[768,3072]{1,0:T(8,128)}, f32[3072,768]{1,0:T(8,128)}) custom-call(s32[5]{0:T(128)} %stack.58.meta_ref, bf16[768,768]{1,0:T(8,128)(2,1)} %collective-permute-done.34.refs_0_, bf16[768,768]{1,0:T(8,128)(2,1)} %copy-done.20, bf16[768,768]{1,0:T(8,128)(2,1)} %collective-permute-done.35.refs_2_, ...), custom_call_target="tpu_custom_call", output_to_operand_aliasing={{0}: (5, {}), {1}: (6, {})} | custom-call | flops 1 | bytes 1 | tf_op jit(solution)/shard_map/widen/pallas_call | solution.py:74
  334.8 6.8 %spread_columns.1 = f32[768,2304]{1,0:T(8,128)} custom-call(s32[5]{0:T(128)} %stack.52.chip_ref.meta_ref, bf16[2,3,384,128]{3,2,1,0:T(8,128)(2,1)} %bitcast.64, bf16[2,3,384,128]{3,2,1,0:T(8,128)(2,1)} %bitcast.25.refs_1_, bf16[2,3,384,128]{3,2,1,0:T(8,128)(2,1)} %bitcast.55, bf16[2,3,384,128]{3,2,1,0:T(8,128)(2,1)} %bitcast.59, ...), custom_call_target="tpu_custom_call" | custom-call | flops 1 | bytes 1 | tf_op jit(solution)/shard_map/spread_columns/pallas_call | solution.py:74
  (222 shorter events, 119.4 us)
Async XLA Ops:
  1.2 22.2 %collective-permute-start = (bf16[512,768]{1,0:T(8,128)(2,1)}, bf16[512,768]{1,0:T(8,128)(2,1)S(1)}, u32[]{:S(2)}, u32[]{:S(2)}) collective-permute-start(bf16[512,768]{1,0:T(8,128)(2,1)} %bitcast.47), channel_id=1, source_target_pairs={{0,8},{4,12},{8,16},{12,20},{16,24},{20,28},{1,9},{5,13},{9,17},{1... | collective-permute-start | bytes 2359304 | tf_op jit(solution)/shard_map/ppermute | solution.py:899
  23.3 30.8 %collective-permute-start.4 = (bf16[256,768]{1,0:T(8,128)(2,1)S(1)}, bf16[256,768]{1,0:T(8,128)(2,1)S(1)}, u32[]{:S(2)}, u32[]{:S(2)}) collective-permute-start(bf16[256,768]{1,0:T(8,128)(2,1)S(1)} %copy-done.45), channel_id=1, source_target_pairs={{0,1},{1,0},{2,3},{3,2},{4,5},{5,4},{6,7},{7,6},{8,9},{9,8},{10,11... | collective-permute-start | bytes 1179656 | tf_op jit(solution)/shard_map/ppermute | solution.py:889
  24.9 29.7 %collective-permute-start.5 = (bf16[256,768]{1,0:T(8,128)(2,1)S(1)}, bf16[256,768]{1,0:T(8,128)(2,1)S(1)}, u32[]{:S(2)}, u32[]{:S(2)}) collective-permute-start(bf16[256,768]{1,0:T(8,128)(2,1)S(1)} %copy-done.44), channel_id=1, source_target_pairs={{0,2},{1,3},{2,0},{3,1},{4,6},{5,7},{6,4},{7,5},{8,10},{9,11},{10,... | collective-permute-start | bytes 1179656 | tf_op jit(solution)/shard_map/ppermute | solution.py:889
  27.5 27.2 %collective-permute-start.6 = (bf16[256,768]{1,0:T(8,128)(2,1)S(1)}, bf16[256,768]{1,0:T(8,128)(2,1)S(1)}, u32[]{:S(2)}, u32[]{:S(2)}) collective-permute-start(bf16[256,768]{1,0:T(8,128)(2,1)S(1)} %copy-done.43), channel_id=1, source_target_pairs={{0,3},{1,2},{2,1},{3,0},{4,7},{5,6},{6,5},{7,4},{8,11},{9,10},{10,... | collective-permute-start | bytes 1179656 | tf_op jit(solution)/shard_map/ppermute | solution.py:889
  62.6 23.2 %collective-permute-start.7 = (bf16[256,768]{1,0:T(8,128)(2,1)}, bf16[256,768]{1,0:T(8,128)(2,1)S(1)}, u32[]{:S(2)}, u32[]{:S(2)}) collective-permute-start(bf16[256,768]{1,0:T(8,128)(2,1)} %get-tuple-element.188), channel_id=1, source_target_pairs={{0,1},{1,0},{2,3},{3,2},{4,5},{5,4},{6,7},{7,6},{8,9},{9,8},{10,11... | collective-permute-start | bytes 1179656 | tf_op jit(solution)/shard_map/ppermute | solution.py:889
  69.5 30.0 %collective-permute-start.8 = (bf16[256,768]{1,0:T(8,128)(2,1)}, bf16[256,768]{1,0:T(8,128)(2,1)S(1)}, u32[]{:S(2)}, u32[]{:S(2)}) collective-permute-start(bf16[256,768]{1,0:T(8,128)(2,1)} %get-tuple-element.192), channel_id=1, source_target_pairs={{0,2},{1,3},{2,0},{3,1},{4,6},{5,7},{6,4},{7,5},{8,10},{9,11},{10,... | collective-permute-start | bytes 1179656 | tf_op jit(solution)/shard_map/ppermute | solution.py:889
  70.6 40.0 %collective-permute-start.9 = (bf16[256,768]{1,0:T(8,128)(2,1)}, bf16[256,768]{1,0:T(8,128)(2,1)S(1)}, u32[]{:S(2)}, u32[]{:S(2)}) collective-permute-start(bf16[256,768]{1,0:T(8,128)(2,1)} %get-tuple-element.196), channel_id=1, source_target_pairs={{0,3},{1,2},{2,1},{3,0},{4,7},{5,6},{6,5},{7,4},{8,11},{9,10},{10,... | collective-permute-start | bytes 1179656 | tf_op jit(solution)/shard_map/ppermute | solution.py:889
  96.7 27.9 %collective-permute-start.10 = (bf16[256,768]{1,0:T(8,128)(2,1)}, bf16[256,768]{1,0:T(8,128)(2,1)S(1)}, u32[]{:S(2)}, u32[]{:S(2)}) collective-permute-start(bf16[256,768]{1,0:T(8,128)(2,1)} %get-tuple-element.193), channel_id=1, source_target_pairs={{0,1},{1,0},{2,3},{3,2},{4,5},{5,4},{6,7},{7,6},{8,9},{9,8},{10,11... | collective-permute-start | bytes 1179656 | tf_op jit(solution)/shard_map/ppermute | solution.py:889
  110.4 30.5 %collective-permute-start.11 = (bf16[256,768]{1,0:T(8,128)(2,1)}, bf16[256,768]{1,0:T(8,128)(2,1)S(1)}, u32[]{:S(2)}, u32[]{:S(2)}) collective-permute-start(bf16[256,768]{1,0:T(8,128)(2,1)} %get-tuple-element.197), channel_id=1, source_target_pairs={{0,2},{1,3},{2,0},{3,1},{4,6},{5,7},{6,4},{7,5},{8,10},{9,11},{10,... | collective-permute-start | bytes 1179656 | tf_op jit(solution)/shard_map/ppermute | solution.py:889
  153.3 45.7 %collective-permute-start.22 = (bf16[768,768]{1,0:T(8,128)(2,1)}, bf16[768,768]{1,0:T(8,128)(2,1)}, u32[]{:S(2)}, u32[]{:S(2)}) collective-permute-start(bf16[768,768]{1,0:T(8,128)(2,1)} %add_convert_fusion), channel_id=1, source_target_pairs={{0,16},{4,20},{8,24},{12,28},{16,0},{20,4},{24,8},{28,12},{1,17},{... | collective-permute-start | bytes 3538952 | tf_op jit(solution)/shard_map/ppermute | solution.py:889
  157.9 41.0 %collective-permute-start.21 = (bf16[768,768]{1,0:T(8,128)(2,1)}, bf16[768,768]{1,0:T(8,128)(2,1)}, u32[]{:S(2)}, u32[]{:S(2)}) collective-permute-start(bf16[768,768]{1,0:T(8,128)(2,1)} %add_convert_fusion.1), channel_id=1, source_target_pairs={{0,8},{4,12},{8,0},{12,4},{16,24},{20,28},{24,16},{28,20},{1,9},{5... | collective-permute-start | bytes 3538952 | tf_op jit(solution)/shard_map/ppermute | solution.py:889
  158.5 38.2 %collective-permute-start.16 = (bf16[256,768]{1,0:T(8,128)(2,1)}, bf16[256,768]{1,0:T(8,128)(2,1)S(1)}, u32[]{:S(2)}, u32[]{:S(2)}) collective-permute-start(bf16[256,768]{1,0:T(8,128)(2,1)} %get-tuple-element.245), channel_id=1, source_target_pairs={{0,1},{1,0},{2,3},{3,2},{4,5},{5,4},{6,7},{7,6},{8,9},{9,8},{10,11... | collective-permute-start | bytes 1179656 | tf_op jit(solution)/shard_map/ppermute | solution.py:889
  163.0 33.8 %collective-permute-start.17 = (bf16[256,768]{1,0:T(8,128)(2,1)}, bf16[256,768]{1,0:T(8,128)(2,1)}, u32[]{:S(2)}, u32[]{:S(2)}) collective-permute-start(bf16[256,768]{1,0:T(8,128)(2,1)} %get-tuple-element.246), channel_id=1, source_target_pairs={{0,2},{1,3},{2,0},{3,1},{4,6},{5,7},{6,4},{7,5},{8,10},{9,11},{10,... | collective-permute-start | bytes 1179656 | tf_op jit(solution)/shard_map/ppermute | solution.py:889
  164.2 32.6 %collective-permute-start.18 = (bf16[256,768]{1,0:T(8,128)(2,1)}, bf16[256,768]{1,0:T(8,128)(2,1)}, u32[]{:S(2)}, u32[]{:S(2)}) collective-permute-start(bf16[256,768]{1,0:T(8,128)(2,1)} %get-tuple-element.247), channel_id=1, source_target_pairs={{0,3},{1,2},{2,1},{3,0},{4,7},{5,6},{6,5},{7,4},{8,11},{9,10},{10,... | collective-permute-start | bytes 1179656 | tf_op jit(solution)/shard_map/ppermute | solution.py:889
  197.6 20.8 %collective-permute-start.20 = (bf16[2304,128]{1,0:T(8,128)(2,1)}, bf16[2304,128]{1,0:T(8,128)(2,1)S(1)}, u32[]{:S(2)}, u32[]{:S(2)}) collective-permute-start(bf16[2304,128]{1,0:T(8,128)(2,1)} %get-tuple-element.250), channel_id=1, source_target_pairs={{0,16},{4,20},{8,24},{12,28},{16,0},{20,4},{24,8},{28,12},{1,17},{... | collective-permute-start | bytes 1769480 | tf_op jit(solution)/shard_map/ppermute | solution.py:889
  201.2 23.4 %collective-permute-start.24 = (bf16[384,768]{1,0:T(8,128)(2,1)}, bf16[384,768]{1,0:T(8,128)(2,1)S(1)}, u32[]{:S(2)}, u32[]{:S(2)}) collective-permute-start(bf16[384,768]{1,0:T(8,128)(2,1)} %add_convert_fusion.7), channel_id=1, source_target_pairs={{0,8},{4,12},{8,0},{12,4},{16,24},{20,28},{24,16},{28,20},{1,9},{5... | collective-permute-start | bytes 1769480 | tf_op jit(solution)/shard_map/ppermute | solution.py:889
  230.0 25.4 %collective-permute-start.29 = (bf16[384,768]{1,0:T(8,128)(2,1)S(1)}, bf16[384,768]{1,0:T(8,128)(2,1)}, u32[]{:S(2)}, u32[]{:S(2)}) collective-permute-start(bf16[384,768]{1,0:T(8,128)(2,1)S(1)} %add_convert_fusion.3), channel_id=1, source_target_pairs={{0,8},{4,12},{8,0},{12,4},{16,24},{20,28},{24,16},{28,20},{1,9},{5... | collective-permute-start | bytes 1769480 | tf_op jit(solution)/shard_map/ppermute | solution.py:889
  237.2 23.4 %all-to-all-start = ((bf16[4,2,288,128]{3,2,1,0:T(8,128)(2,1)}), bf16[4,2,288,128]{3,2,1,0:T(8,128)(2,1)S(1)}, u32[]{:S(2)}, u32[]{:S(2)}) async-start(bf16[4,2,288,128]{3,2,1,0:T(8,128)(2,1)} %pad_maximum_fusion.2), calls=%async_computation | async-start | bytes 1179648 | tf_op jit(solution)/shard_map/all_to_all | solution.py:893
  264.3 28.8 %collective-permute-start.34 = (bf16[768,768]{1,0:T(8,128)(2,1)S(1)}, bf16[768,768]{1,0:T(8,128)(2,1)}, u32[]{:S(2)}, u32[]{:S(2)}) collective-permute-start(bf16[768,768]{1,0:T(8,128)(2,1)S(1)} %pad_maximum_fusion.refs_0_), channel_id=1, source_target_pairs={{0,4},{4,0},{8,12},{12,8},{16,20},{20,16},{24,28},{28,24},{1,5},{5... | collective-permute-start | bytes 3538952 | tf_op jit(solution)/shard_map/ppermute | solution.py:889
  264.4 28.7 %collective-permute-start.35 = (bf16[768,768]{1,0:T(8,128)(2,1)S(1)}, bf16[768,768]{1,0:T(8,128)(2,1)}, u32[]{:S(2)}, u32[]{:S(2)}) collective-permute-start(bf16[768,768]{1,0:T(8,128)(2,1)S(1)} %pad_maximum_fusion.1.refs_2_), channel_id=1, source_target_pairs={{0,4},{4,0},{8,12},{12,8},{16,20},{20,16},{24,28},{28,24},{1,5},{5... | collective-permute-start | bytes 3538952 | tf_op jit(solution)/shard_map/ppermute | solution.py:889
  264.9 28.2 %collective-permute-start.33 = (bf16[768,768]{1,0:T(8,128)(2,1)S(1)}, bf16[768,768]{1,0:T(8,128)(2,1)}, u32[]{:S(2)}, u32[]{:S(2)}) collective-permute-start(bf16[768,768]{1,0:T(8,128)(2,1)S(1)} %pad_maximum_fusion.1.refs_2_), channel_id=1, source_target_pairs={{0,16},{4,20},{8,24},{12,28},{16,0},{20,4},{24,8},{28,12},{1,17},{... | collective-permute-start | bytes 3538952 | tf_op jit(solution)/shard_map/ppermute | solution.py:889
  266.6 27.8 %collective-permute-start.32 = (bf16[768,768]{1,0:T(8,128)(2,1)S(1)}, bf16[768,768]{1,0:T(8,128)(2,1)}, u32[]{:S(2)}, u32[]{:S(2)}) collective-permute-start(bf16[768,768]{1,0:T(8,128)(2,1)S(1)} %pad_maximum_fusion.refs_0_), channel_id=1, source_target_pairs={{0,8},{4,12},{8,0},{12,4},{16,24},{20,28},{24,16},{28,20},{1,9},{5... | collective-permute-start | bytes 3538952 | tf_op jit(solution)/shard_map/ppermute | solution.py:889
  268.2 24.9 %all-to-all-start.1 = ((bf16[4,2,288,128]{3,2,1,0:T(8,128)(2,1)}), bf16[4,2,288,128]{3,2,1,0:T(8,128)(2,1)S(1)}, u32[]{:S(2)}, u32[]{:S(2)}) async-start(bf16[4,2,288,128]{3,2,1,0:T(8,128)(2,1)} %broadcast_in_dim.16), calls=%async_computation.1 | async-start | bytes 1179648 | tf_op jit(solution)/shard_map/all_to_all | solution.py:893
  313.4 28.8 %collective-permute-start.31 = (bf16[512,768]{1,0:T(8,128)(2,1)}, bf16[512,768]{1,0:T(8,128)(2,1)}, u32[]{:S(2)}, u32[]{:S(2)}) collective-permute-start(bf16[512,768]{1,0:T(8,128)(2,1)} %add_convert_fusion.2), channel_id=1, source_target_pairs={{8,0},{12,4},{16,8},{20,12},{24,16},{28,20},{9,1},{13,5},{17,9},{2... | collective-permute-start | bytes 2359304 | tf_op jit(solution)/shard_map/ppermute | solution.py:899
  (74 other events, 746.9 us)

commit v2 on v1

--- a/solution.py
+++ b/solution.py
@@ -1162,13 +1162,13 @@
     small = jnp.concatenate([gain_one_grad, bias_one_grad, gain_two_grad, bias_two_grad], axis=0)
     (give,) = meet([dense, experts], (give,))
     near = swap(give, "seq", 1)
-    (near,) = meet([dense], (near,))
+    hops = [("seq", bit) for bit in [1] + bits]
+    hops += [("exp", 1 << b) for b in range(sources.bit_length() - 1)]
+    small = Stream(small_steps(small, hops))
+    (near,) = meet([dense, small], (near,))
     for rest in range(len(bits) - 2):
         meet([dense, experts])
     far = add(halo, near[local_len:])
-    hops = [("seq", bit) for bit in bits + [1]]
-    hops += [("exp", 1 << b) for b in range(sources.bit_length() - 1)]
-    small = Stream(small_steps(small, hops))
     layer_output = finish(slot, resid, returned)
     layer_output, far = meet([dense, experts, small], (layer_output, far))
     far = shift(far, "seq", -2)

time: 348 us -> 349 us (level)
  Pallas kernels: 184 us -> 179 us
    ppermute x48, starting transfers between devices: 54.3 us -> 59.8 us  [swap(): lax.ppermute(block, axis, [(i, i ^ distance) for i in range(lax.axis_size...]
    pallas_call x20, Pallas kernels: 184 us -> 179 us  [call(): pl.pallas_call(body, name=name, out_shape=out_shape, grid_spec=pltpu.Pref...]
    unnamed x92 -> x98, local copies, waits for them, and re-layouts: 9.87 us -> 11.3 us
  transfers between devices with their start and end apart: 52 -> 52, of which waited for: 16 -> 15; matrix products, arithmetic and copies ran while one was open for 6% -> 6% of each run, Pallas kernels for 50% -> 49%
where the time goes in v2:
time: 349 us; the launch traced here: 347 us
  Pallas kernels  179 us (51%)
  starting transfers between devices  73.8 us (21%)
  waiting for transfers between devices  57.7 us (17%)
  other arithmetic  19.4 us (6%)
  local copies, waits for them, and re-layouts  15.5 us (4%)
    pallas_call x20, Pallas kernels, call(): pl.pallas_call(body, name=name, out_shape=out_shape, grid_spec=pltpu.Pref...  179 us
    ppermute x48, starting transfers between devices, swap(): lax.ppermute(block, axis, [(i, i ^ distance) for i in range(lax.axis_size...  59.8 us
    ppermute x48, waiting for transfers between devices, swap(): lax.ppermute(block, axis, [(i, i ^ distance) for i in range(lax.axis_size...  54.9 us
    convert_element_type x10, other arithmetic, total(): return sum((t.astype(F32) for t in terms)).astype(BF16)  12.7 us
    unnamed x98, local copies, waits for them, and re-layouts  11.3 us
    all_to_all x2, starting transfers between devices, trade(): return lax.all_to_all(block, axis, split_axis=0, concat_axis=0, tiled=True)  8.25 us
  transfers between devices with their start and end apart: 52, of which 15 were waited for; matrix products, arithmetic and copies ran while one was open for 6% of the time, Pallas kernels for 49%

profile of v2, /device:TPU:0, one launch (start us, length us, event | category | flops | bytes accessed | tf_op | source)
XLA Modules:
  0.0 347.0 jit_solution(11160648329015072653)
XLA Ops:
  1.2 4.5 %collective-permute-start = (bf16[512,768]{1,0:T(8,128)(2,1)}, bf16[512,768]{1,0:T(8,128)(2,1)S(1)}, u32[]{:S(2)}, u32[]{:S(2)}) collective-permute-start(bf16[512,768]{1,0:T(8,128)(2,1)} %bitcast.47), channel_id=1, source_target_pairs={{0,8},{4,12},{8,16},{12,20},{16,24},{20,28},{1,9},{5,13},{9,17},{1... | collective-permute-start | bytes 2359304 | tf_op jit(solution)/shard_map/ppermute | solution.py:899
  7.6 5.0 %route.1 = (s32[512,1]{1,0:T(8,128)}, s32[1,1024]{1,0:T(1,128)}, s32[1024,1]{1,0:T(8,128)}, s32[1,128]{1,0:T(1,128)}, bf16[256,768]{1,0:T(8,128)(2,1)}, /*index=...) custom-call(s32[3]{0:T(128)} %pad_add_fusion.at_ref, s32[1,512]{1,0:T(1,128)} %ids_ref.1, ...), custom_call_target="tpu_custom_call" | custom-call | flops 1 | bytes 1 | tf_op jit(solution)/shard_map/route/pallas_call | solution.py:74
  14.8 7.6 %project.2 = (bf16[2048,768]{1,0:T(8,128)(2,1)}, bf16[2048,384]{1,0:T(8,128)(2,1)}, bf16[2048,384]{1,0:T(8,128)(2,1)}, bf16[1024,384]{1,0:T(8,128)(2,1)}) custom-call(s32[1]{0:T(128)} %bitcast.core_ref, bf16[512,768]{1,0:T(8,128)(2,1)} %bitcast.48, bf16[512,768]{1,0:T(8,128)(2,1)} %copy-done.6, f32[24,128]{1,0:T(8,128)} %pad_maximum_fusion.5.norm_ref, ...), custom_call_target="tpu_custom_call" | custom-call | flops 1 | bytes 1 | tf_op jit(solution)/shard_map/project/pallas_call | solution.py:74
  28.6 6.5 %project.3 = (bf16[2048,768]{1,0:T(8,128)(2,1)}, bf16[2048,384]{1,0:T(8,128)(2,1)}, bf16[2048,384]{1,0:T(8,128)(2,1)}) custom-call(s32[1]{0:T(128)} %bitcast.core_ref, bf16[512,768]{1,0:T(8,128)(2,1)} %copy-done.4, bf16[512,768]{1,0:T(8,128)(2,1)} %copy-done.5, ...), custom_call_target="tpu_custom_call", output_to_operand_aliasing={{0}: (7, {}), {1}: (8, {}), {2}: (9, {})} | custom-call | flops 1 | bytes 1 | tf_op jit(solution)/shard_map/project/pallas_call | solution.py:74
  35.1 16.8 %attend.1 = (bf16[512,384]{1,0:T(8,128)(2,1)}, bf16[512,384]{1,0:T(8,128)(2,1)}, bf16[1024,384]{1,0:T(8,128)(2,1)}, f32[384,1024]{1,0:T(8,128)}, f32[8,1024]{1,0:T(8,128)}) custom-call(s32[1,128]{1,0:T(1,128)} %get-tuple-element.175.meta_ref, bf16[1024,384]{1,0:T(8,128)(2,1)} %get-tuple-element.169.q_ref.q_hbm, ...), custom_call_target="tpu_custom_call" | custom-call | flops 1 | bytes 1 | tf_op jit(solution)/shard_map/attend/pallas_call | solution.py:74
  55.5 5.8 %lift.1 = (f32[512,768]{1,0:T(8,128)}, bf16[256,768]{1,0:T(8,128)(2,1)}, bf16[256,768]{1,0:T(8,128)(2,1)}, bf16[256,768]{1,0:T(8,128)(2,1)}, bf16[256,768]{1,0:T(8,128)(2,1)}) custom-call(s32[1]{0:T(128)} %bitcast.core_ref, bf16[512,384]{1,0:T(8,128)(2,1)} %get-tuple-element.179.own_ref, bf16[512,384]{1,0:T(8,128)(2,1)} %copy-done.37, ...), custom_call_target="tpu_custom_call" | custom-call | flops 1 | bytes 1 | tf_op jit(solution)/shard_map/lift/pallas_call | solution.py:74
  61.3 8.3 %collective-permute-start.7 = (bf16[256,768]{1,0:T(8,128)(2,1)}, bf16[256,768]{1,0:T(8,128)(2,1)S(1)}, u32[]{:S(2)}, u32[]{:S(2)}) collective-permute-start(bf16[256,768]{1,0:T(8,128)(2,1)} %get-tuple-element.189), channel_id=1, source_target_pairs={{0,1},{1,0},{2,3},{3,2},{4,5},{5,4},{6,7},{7,6},{8,9},{9,8},{10,11... | collective-permute-start | bytes 1179656 | tf_op jit(solution)/shard_map/ppermute | solution.py:889
  72.0 10.1 %expert.4 = (bf16[3072,256]{1,0:T(8,128)(2,1)}, bf16[256,3072]{1,0:T(8,128)(2,1)}, bf16[256,768]{1,0:T(8,128)(2,1)}, bf16[256,768]{1,0:T(8,128)(2,1)}, bf16[768,256]{1,0:T(8,128)(2,1)}) custom-call(bf16[256,768]{1,0:T(8,128)(2,1)} %get-tuple-element.187.rows_ref, bf16[256,768]{1,0:T(8,128)(2,1)} %get-tuple-element.181.grad_ref.refs_4_, ...), custom_call_target="tpu_custom_call" | custom-call | flops 1 | bytes 1 | tf_op jit(solution)/shard_map/expert/pallas_call | solution.py:74
  86.6 10.1 %expert.5 = (bf16[3072,256]{1,0:T(8,128)(2,1)}, bf16[256,3072]{1,0:T(8,128)(2,1)}, bf16[256,768]{1,0:T(8,128)(2,1)}, bf16[256,768]{1,0:T(8,128)(2,1)}, bf16[768,256]{1,0:T(8,128)(2,1)}) custom-call(bf16[256,768]{1,0:T(8,128)(2,1)} %copy-done.32, bf16[256,768]{1,0:T(8,128)(2,1)} %copy-done.16, bf16[768,3072]{1,0:T(8,128)(2,1)} %bitcast.39, ...), custom_call_target="tpu_custom_call" | custom-call | flops 1 | bytes 1 | tf_op jit(solution)/shard_map/expert/pallas_call | solution.py:74
  100.3 10.1 %expert.6 = (bf16[3072,256]{1,0:T(8,128)(2,1)}, bf16[256,3072]{1,0:T(8,128)(2,1)}, bf16[256,768]{1,0:T(8,128)(2,1)}, bf16[256,768]{1,0:T(8,128)(2,1)}, bf16[768,256]{1,0:T(8,128)(2,1)}) custom-call(bf16[256,768]{1,0:T(8,128)(2,1)} %copy-done.31, bf16[256,768]{1,0:T(8,128)(2,1)} %copy-done.17, bf16[768,3072]{1,0:T(8,128)(2,1)} %bitcast.40, ...), custom_call_target="tpu_custom_call" | custom-call | flops 1 | bytes 1 | tf_op jit(solution)/shard_map/expert/pallas_call | solution.py:74
  111.3 10.2 %expert.7 = (bf16[3072,256]{1,0:T(8,128)(2,1)}, bf16[256,3072]{1,0:T(8,128)(2,1)}, bf16[256,768]{1,0:T(8,128)(2,1)}, bf16[256,768]{1,0:T(8,128)(2,1)}, bf16[768,256]{1,0:T(8,128)(2,1)}) custom-call(bf16[256,768]{1,0:T(8,128)(2,1)} %copy-done.30, bf16[256,768]{1,0:T(8,128)(2,1)} %copy-done.18, bf16[768,3072]{1,0:T(8,128)(2,1)} %bitcast.41, ...), custom_call_target="tpu_custom_call" | custom-call | flops 1 | bytes 1 | tf_op jit(solution)/shard_map/expert/pallas_call | solution.py:74
  124.7 16.3 %expert_grad.1 = (bf16[1536,768]{1,0:T(8,128)(2,1)}, bf16[1536,768]{1,0:T(8,128)(2,1)}, bf16[1536,768]{1,0:T(8,128)(2,1)}, bf16[1536,768]{1,0:T(8,128)(2,1)}) custom-call(s32[5]{0:T(128)} %stack.52.chip_ref.meta_ref, bf16[768,256]{1,0:T(8,128)(2,1)} %get-tuple-element.203.refs_0_, bf16[768,256]{1,0:T(8,128)(2,1)} %get-tuple-element.204.refs_1_, ...), custom_call_target="tpu_custom_call" | custom-call | flops 1 | bytes 1 | tf_op jit(solution)/shard_map/expert_grad/pallas_call | solution.py:74
  141.9 5.3 %lower.1 = (f32[512,768]{1,0:T(8,128)}, bf16[512,768]{1,0:T(8,128)(2,1)}, f32[1,768]{1,0:T(1,128)}, f32[1,768]{1,0:T(1,128)}) custom-call(s32[512,1]{1,0:T(8,128)} %get-tuple-element.167.slot_ref, f32[512,768]{1,0:T(8,128)} %get-tuple-element.186.resid_ref, bf16[512,768]{1,0:T(8,128)(2,1)} %bitcast.57, f32[24,128]{1,0:T(8,128)} %pad_maximum_fusion.5.norm_ref, ...), custom_call_target="tpu_custom_call" | custom-call | flops 1 | bytes 1 | tf_op jit(solution)/shard_map/lower/pallas_call | solution.py:74
  165.1 18.5 %attend_back.1 = (bf16[1024,384]{1,0:T(8,128)(2,1)}, bf16[2048,384]{1,0:T(8,128)(2,1)}, bf16[2048,384]{1,0:T(8,128)(2,1)}) custom-call(s32[1,128]{1,0:T(1,128)} %get-tuple-element.175.meta_ref, bf16[1024,384]{1,0:T(8,128)(2,1)} %get-tuple-element.169.q_ref.q_hbm, bf16[2048,384]{1,0:T(8,128)(2,1)} %get-tuple-element.176.k_ref.k_hbm, ...), custom_call_target="tpu_custom_call" | custom-call | flops 1 | bytes 1 | tf_op jit(solution)/shard_map/attend_back/pallas_call | solution.py:74
  183.6 10.1 %dense.1 = (bf16[2304,128]{1,0:T(8,128)(2,1)}, bf16[2304,128]{1,0:T(8,128)(2,1)}, bf16[2304,128]{1,0:T(8,128)(2,1)}, bf16[2304,128]{1,0:T(8,128)(2,1)}) custom-call(s32[5]{0:T(128)} %stack.52.chip_ref.meta_ref, bf16[2048,768]{1,0:T(8,128)(2,1)} %get-tuple-element.174.a_hbm, bf16[1024,384]{1,0:T(8,128)(2,1)} %get-tuple-element.256.gq_hbm.gq_ref, ...), custom_call_target="tpu_custom_call" | custom-call | flops 1 | bytes 1 | tf_op jit(solution)/shard_map/dense/pallas_call | solution.py:74
  198.9 4.8 %collective-permute-start.20 = (bf16[2304,128]{1,0:T(8,128)(2,1)}, bf16[2304,128]{1,0:T(8,128)(2,1)S(1)}, u32[]{:S(2)}, u32[]{:S(2)}) collective-permute-start(bf16[2304,128]{1,0:T(8,128)(2,1)} %get-tuple-element.251), channel_id=1, source_target_pairs={{0,16},{4,20},{8,24},{12,28},{16,0},{20,4},{24,8},{28,12},{1,17},{... | collective-permute-start | bytes 1769480 | tf_op jit(solution)/shard_map/ppermute | solution.py:889
  207.4 13.2 %project_back.1 = (f32[512,768]{1,0:T(8,128)}, bf16[1024,768]{1,0:T(8,128)(2,1)}, f32[512,768]{1,0:T(8,128)}, f32[1,768]{1,0:T(1,128)}, f32[1,768]{1,0:T(1,128)}) custom-call(s32[1]{0:T(128)} %bitcast.core_ref, bf16[512,768]{1,0:T(8,128)(2,1)} %bitcast.50, bf16[512,768]{1,0:T(8,128)(2,1)} %copy-done.6, bf16[512,768]{1,0:T(8,128)(2,1)} %copy-done.4, ...), custom_call_target="tpu_custom_call" | custom-call | flops 1 | bytes 1 | tf_op jit(solution)/shard_map/project_back/pallas_call | solution.py:74
  224.3 4.8 %collective-permute-done.23 = bf16[384,768]{1,0:T(8,128)(2,1)S(1)} collective-permute-done((bf16[384,768]{1,0:T(8,128)(2,1)S(1)}, bf16[384,768]{1,0:T(8,128)(2,1)S(1)}, u32[]{:S(2)}, u32[]{:S(2)}) %collective-permute-start.23) | collective-permute-done | bytes 589856 | tf_op jit(solution)/shard_map/ppermute | solution.py:889
  254.8 6.0 %collective-permute-done.29 = bf16[384,768]{1,0:T(8,128)(2,1)S(1)} collective-permute-done((bf16[384,768]{1,0:T(8,128)(2,1)S(1)}, bf16[384,768]{1,0:T(8,128)(2,1)S(1)}, u32[]{:S(2)}, u32[]{:S(2)}) %collective-permute-start.29) | collective-permute-done | bytes 589856 | tf_op jit(solution)/shard_map/ppermute | solution.py:889
  268.5 4.8 %all-to-all-start.1 = ((bf16[4,2,288,128]{3,2,1,0:T(8,128)(2,1)}), bf16[4,2,288,128]{3,2,1,0:T(8,128)(2,1)S(1)}, u32[]{:S(2)}, u32[]{:S(2)}) async-start(bf16[4,2,288,128]{3,2,1,0:T(8,128)(2,1)} %broadcast_in_dim.16), calls=%async_computation.1 | async-start | bytes 1179648 | tf_op jit(solution)/shard_map/all_to_all | solution.py:893
  274.4 19.0 %collective-permute-done.37 = f32[4,768]{1,0:T(4,128)S(1)} collective-permute-done((f32[4,768]{1,0:T(4,128)S(1)}, f32[4,768]{1,0:T(4,128)S(1)}, u32[]{:S(2)}, u32[]{:S(2)}) %collective-permute-start.37) | collective-permute-done | bytes 12320 | tf_op jit(solution)/shard_map/ppermute | solution.py:889
  299.8 7.5 %widen.2 = (f32[768,3072]{1,0:T(8,128)}, f32[3072,768]{1,0:T(8,128)}) custom-call(s32[5]{0:T(128)} %stack.52.chip_ref.meta_ref, bf16[768,768]{1,0:T(8,128)(2,1)} %copy-done.2, bf16[768,768]{1,0:T(8,128)(2,1)} %collective-permute-done.33.refs_1_, bf16[768,768]{1,0:T(8,128)(2,1)} %copy-done.1, bf16[768,768]{1,0:T(8,128)(2,1)} %collective-permute-done.34.refs_3_), custom_call_target="tpu_custom_call" | custom-call | flops 1 | bytes 1 | tf_op jit(solution)/shard_map/widen/pallas_call | solution.py:74
  317.9 7.6 %widen.3 = (f32[768,3072]{1,0:T(8,128)}, f32[3072,768]{1,0:T(8,128)}) custom-call(s32[5]{0:T(128)} %stack.58.meta_ref, bf16[768,768]{1,0:T(8,128)(2,1)} %collective-permute-done.35.refs_0_, bf16[768,768]{1,0:T(8,128)(2,1)} %copy-done.20, bf16[768,768]{1,0:T(8,128)(2,1)} %collective-permute-done.36.refs_2_, ...), custom_call_target="tpu_custom_call", output_to_operand_aliasing={{0}: (5, {}), {1}: (6, {})} | custom-call | flops 1 | bytes 1 | tf_op jit(solution)/shard_map/widen/pallas_call | solution.py:74
  334.3 6.8 %spread_columns.1 = f32[768,2304]{1,0:T(8,128)} custom-call(s32[5]{0:T(128)} %stack.52.chip_ref.meta_ref, bf16[2,3,384,128]{3,2,1,0:T(8,128)(2,1)} %bitcast.64, bf16[2,3,384,128]{3,2,1,0:T(8,128)(2,1)} %bitcast.25.refs_1_, bf16[2,3,384,128]{3,2,1,0:T(8,128)(2,1)} %bitcast.55, bf16[2,3,384,128]{3,2,1,0:T(8,128)(2,1)} %bitcast.59, ...), custom_call_target="tpu_custom_call" | custom-call | flops 1 | bytes 1 | tf_op jit(solution)/shard_map/spread_columns/pallas_call | solution.py:74
  (228 shorter events, 126.0 us)
Async XLA Ops:
  1.2 22.2 %collective-permute-start = (bf16[512,768]{1,0:T(8,128)(2,1)}, bf16[512,768]{1,0:T(8,128)(2,1)S(1)}, u32[]{:S(2)}, u32[]{:S(2)}) collective-permute-start(bf16[512,768]{1,0:T(8,128)(2,1)} %bitcast.47), channel_id=1, source_target_pairs={{0,8},{4,12},{8,16},{12,20},{16,24},{20,28},{1,9},{5,13},{9,17},{1... | collective-permute-start | bytes 2359304 | tf_op jit(solution)/shard_map/ppermute | solution.py:899
  23.3 28.6 %collective-permute-start.4 = (bf16[256,768]{1,0:T(8,128)(2,1)S(1)}, bf16[256,768]{1,0:T(8,128)(2,1)S(1)}, u32[]{:S(2)}, u32[]{:S(2)}) collective-permute-start(bf16[256,768]{1,0:T(8,128)(2,1)S(1)} %copy-done.48), channel_id=1, source_target_pairs={{0,1},{1,0},{2,3},{3,2},{4,5},{5,4},{6,7},{7,6},{8,9},{9,8},{10,11... | collective-permute-start | bytes 1179656 | tf_op jit(solution)/shard_map/ppermute | solution.py:889
  24.9 29.7 %collective-permute-start.5 = (bf16[256,768]{1,0:T(8,128)(2,1)S(1)}, bf16[256,768]{1,0:T(8,128)(2,1)S(1)}, u32[]{:S(2)}, u32[]{:S(2)}) collective-permute-start(bf16[256,768]{1,0:T(8,128)(2,1)S(1)} %copy-done.47), channel_id=1, source_target_pairs={{0,2},{1,3},{2,0},{3,1},{4,6},{5,7},{6,4},{7,5},{8,10},{9,11},{10,... | collective-permute-start | bytes 1179656 | tf_op jit(solution)/shard_map/ppermute | solution.py:889
  27.5 27.2 %collective-permute-start.6 = (bf16[256,768]{1,0:T(8,128)(2,1)S(1)}, bf16[256,768]{1,0:T(8,128)(2,1)S(1)}, u32[]{:S(2)}, u32[]{:S(2)}) collective-permute-start(bf16[256,768]{1,0:T(8,128)(2,1)S(1)} %copy-done.46), channel_id=1, source_target_pairs={{0,3},{1,2},{2,1},{3,0},{4,7},{5,6},{6,5},{7,4},{8,11},{9,10},{10,... | collective-permute-start | bytes 1179656 | tf_op jit(solution)/shard_map/ppermute | solution.py:889
  61.3 24.6 %collective-permute-start.7 = (bf16[256,768]{1,0:T(8,128)(2,1)}, bf16[256,768]{1,0:T(8,128)(2,1)S(1)}, u32[]{:S(2)}, u32[]{:S(2)}) collective-permute-start(bf16[256,768]{1,0:T(8,128)(2,1)} %get-tuple-element.189), channel_id=1, source_target_pairs={{0,1},{1,0},{2,3},{3,2},{4,5},{5,4},{6,7},{7,6},{8,9},{9,8},{10,11... | collective-permute-start | bytes 1179656 | tf_op jit(solution)/shard_map/ppermute | solution.py:889
  69.5 30.0 %collective-permute-start.8 = (bf16[256,768]{1,0:T(8,128)(2,1)}, bf16[256,768]{1,0:T(8,128)(2,1)S(1)}, u32[]{:S(2)}, u32[]{:S(2)}) collective-permute-start(bf16[256,768]{1,0:T(8,128)(2,1)} %get-tuple-element.193), channel_id=1, source_target_pairs={{0,2},{1,3},{2,0},{3,1},{4,6},{5,7},{6,4},{7,5},{8,10},{9,11},{10,... | collective-permute-start | bytes 1179656 | tf_op jit(solution)/shard_map/ppermute | solution.py:889
  70.6 40.0 %collective-permute-start.9 = (bf16[256,768]{1,0:T(8,128)(2,1)}, bf16[256,768]{1,0:T(8,128)(2,1)S(1)}, u32[]{:S(2)}, u32[]{:S(2)}) collective-permute-start(bf16[256,768]{1,0:T(8,128)(2,1)} %get-tuple-element.197), channel_id=1, source_target_pairs={{0,3},{1,2},{2,1},{3,0},{4,7},{5,6},{6,5},{7,4},{8,11},{9,10},{10,... | collective-permute-start | bytes 1179656 | tf_op jit(solution)/shard_map/ppermute | solution.py:889
  96.7 28.0 %collective-permute-start.10 = (bf16[256,768]{1,0:T(8,128)(2,1)}, bf16[256,768]{1,0:T(8,128)(2,1)S(1)}, u32[]{:S(2)}, u32[]{:S(2)}) collective-permute-start(bf16[256,768]{1,0:T(8,128)(2,1)} %get-tuple-element.194), channel_id=1, source_target_pairs={{0,1},{1,0},{2,3},{3,2},{4,5},{5,4},{6,7},{7,6},{8,9},{9,8},{10,11... | collective-permute-start | bytes 1179656 | tf_op jit(solution)/shard_map/ppermute | solution.py:889
  110.4 30.6 %collective-permute-start.11 = (bf16[256,768]{1,0:T(8,128)(2,1)}, bf16[256,768]{1,0:T(8,128)(2,1)S(1)}, u32[]{:S(2)}, u32[]{:S(2)}) collective-permute-start(bf16[256,768]{1,0:T(8,128)(2,1)} %get-tuple-element.198), channel_id=1, source_target_pairs={{0,2},{1,3},{2,0},{3,1},{4,6},{5,7},{6,4},{7,5},{8,10},{9,11},{10,... | collective-permute-start | bytes 1179656 | tf_op jit(solution)/shard_map/ppermute | solution.py:889
  153.4 50.4 %collective-permute-start.22 = (bf16[768,768]{1,0:T(8,128)(2,1)}, bf16[768,768]{1,0:T(8,128)(2,1)}, u32[]{:S(2)}, u32[]{:S(2)}) collective-permute-start(bf16[768,768]{1,0:T(8,128)(2,1)} %add_convert_fusion), channel_id=1, source_target_pairs={{0,16},{4,20},{8,24},{12,28},{16,0},{20,4},{24,8},{28,12},{1,17},{... | collective-permute-start | bytes 3538952 | tf_op jit(solution)/shard_map/ppermute | solution.py:889
  158.0 45.7 %collective-permute-start.21 = (bf16[768,768]{1,0:T(8,128)(2,1)}, bf16[768,768]{1,0:T(8,128)(2,1)}, u32[]{:S(2)}, u32[]{:S(2)}) collective-permute-start(bf16[768,768]{1,0:T(8,128)(2,1)} %add_convert_fusion.1), channel_id=1, source_target_pairs={{0,8},{4,12},{8,0},{12,4},{16,24},{20,28},{24,16},{28,20},{1,9},{5... | collective-permute-start | bytes 3538952 | tf_op jit(solution)/shard_map/ppermute | solution.py:889
  158.6 35.1 %collective-permute-start.16 = (bf16[256,768]{1,0:T(8,128)(2,1)}, bf16[256,768]{1,0:T(8,128)(2,1)S(1)}, u32[]{:S(2)}, u32[]{:S(2)}) collective-permute-start(bf16[256,768]{1,0:T(8,128)(2,1)} %get-tuple-element.246), channel_id=1, source_target_pairs={{0,1},{1,0},{2,3},{3,2},{4,5},{5,4},{6,7},{7,6},{8,9},{9,8},{10,11... | collective-permute-start | bytes 1179656 | tf_op jit(solution)/shard_map/ppermute | solution.py:889
  162.4 31.4 %collective-permute-start.17 = (bf16[256,768]{1,0:T(8,128)(2,1)}, bf16[256,768]{1,0:T(8,128)(2,1)}, u32[]{:S(2)}, u32[]{:S(2)}) collective-permute-start(bf16[256,768]{1,0:T(8,128)(2,1)} %get-tuple-element.247), channel_id=1, source_target_pairs={{0,2},{1,3},{2,0},{3,1},{4,6},{5,7},{6,4},{7,5},{8,10},{9,11},{10,... | collective-permute-start | bytes 1179656 | tf_op jit(solution)/shard_map/ppermute | solution.py:889
  163.5 30.2 %collective-permute-start.18 = (bf16[256,768]{1,0:T(8,128)(2,1)}, bf16[256,768]{1,0:T(8,128)(2,1)}, u32[]{:S(2)}, u32[]{:S(2)}) collective-permute-start(bf16[256,768]{1,0:T(8,128)(2,1)} %get-tuple-element.248), channel_id=1, source_target_pairs={{0,3},{1,2},{2,1},{3,0},{4,7},{5,6},{6,5},{7,4},{8,11},{9,10},{10,... | collective-permute-start | bytes 1179656 | tf_op jit(solution)/shard_map/ppermute | solution.py:889
  194.5 26.1 %collective-permute-start.19 = (bf16[2304,128]{1,0:T(8,128)(2,1)}, bf16[2304,128]{1,0:T(8,128)(2,1)S(1)}, u32[]{:S(2)}, u32[]{:S(2)}) collective-permute-start(bf16[2304,128]{1,0:T(8,128)(2,1)} %get-tuple-element.250), channel_id=1, source_target_pairs={{0,8},{4,12},{8,0},{12,4},{16,24},{20,28},{24,16},{28,20},{1,9},{5... | collective-permute-start | bytes 1769480 | tf_op jit(solution)/shard_map/ppermute | solution.py:889
  198.9 21.7 %collective-permute-start.20 = (bf16[2304,128]{1,0:T(8,128)(2,1)}, bf16[2304,128]{1,0:T(8,128)(2,1)S(1)}, u32[]{:S(2)}, u32[]{:S(2)}) collective-permute-start(bf16[2304,128]{1,0:T(8,128)(2,1)} %get-tuple-element.251), channel_id=1, source_target_pairs={{0,16},{4,20},{8,24},{12,28},{16,0},{20,4},{24,8},{28,12},{1,17},{... | collective-permute-start | bytes 1769480 | tf_op jit(solution)/shard_map/ppermute | solution.py:889
  207.3 21.8 %collective-permute-start.23 = (bf16[384,768]{1,0:T(8,128)(2,1)S(1)}, bf16[384,768]{1,0:T(8,128)(2,1)S(1)}, u32[]{:S(2)}, u32[]{:S(2)}) collective-permute-start(bf16[384,768]{1,0:T(8,128)(2,1)S(1)} %add_convert_fusion.8), channel_id=1, source_target_pairs={{0,16},{4,20},{8,24},{12,28},{16,0},{20,4},{24,8},{28,12},{1,17},{... | collective-permute-start | bytes 1769480 | tf_op jit(solution)/shard_map/ppermute | solution.py:889
  241.7 20.6 %all-to-all-start = ((bf16[4,2,288,128]{3,2,1,0:T(8,128)(2,1)}), bf16[4,2,288,128]{3,2,1,0:T(8,128)(2,1)S(1)}, u32[]{:S(2)}, u32[]{:S(2)}) async-start(bf16[4,2,288,128]{3,2,1,0:T(8,128)(2,1)} %pad_maximum_fusion.2), calls=%async_computation | async-start | bytes 1179648 | tf_op jit(solution)/shard_map/all_to_all | solution.py:893
  264.6 28.8 %collective-permute-start.35 = (bf16[768,768]{1,0:T(8,128)(2,1)S(1)}, bf16[768,768]{1,0:T(8,128)(2,1)}, u32[]{:S(2)}, u32[]{:S(2)}) collective-permute-start(bf16[768,768]{1,0:T(8,128)(2,1)S(1)} %pad_maximum_fusion.refs_0_), channel_id=1, source_target_pairs={{0,4},{4,0},{8,12},{12,8},{16,20},{20,16},{24,28},{28,24},{1,5},{5... | collective-permute-start | bytes 3538952 | tf_op jit(solution)/shard_map/ppermute | solution.py:889
  264.6 28.7 %collective-permute-start.36 = (bf16[768,768]{1,0:T(8,128)(2,1)S(1)}, bf16[768,768]{1,0:T(8,128)(2,1)}, u32[]{:S(2)}, u32[]{:S(2)}) collective-permute-start(bf16[768,768]{1,0:T(8,128)(2,1)S(1)} %pad_maximum_fusion.1.refs_2_), channel_id=1, source_target_pairs={{0,4},{4,0},{8,12},{12,8},{16,20},{20,16},{24,28},{28,24},{1,5},{5... | collective-permute-start | bytes 3538952 | tf_op jit(solution)/shard_map/ppermute | solution.py:889
  265.1 28.2 %collective-permute-start.34 = (bf16[768,768]{1,0:T(8,128)(2,1)S(1)}, bf16[768,768]{1,0:T(8,128)(2,1)}, u32[]{:S(2)}, u32[]{:S(2)}) collective-permute-start(bf16[768,768]{1,0:T(8,128)(2,1)S(1)} %pad_maximum_fusion.1.refs_2_), channel_id=1, source_target_pairs={{0,16},{4,20},{8,24},{12,28},{16,0},{20,4},{24,8},{28,12},{1,17},{... | collective-permute-start | bytes 3538952 | tf_op jit(solution)/shard_map/ppermute | solution.py:889
  266.9 27.8 %collective-permute-start.33 = (bf16[768,768]{1,0:T(8,128)(2,1)S(1)}, bf16[768,768]{1,0:T(8,128)(2,1)}, u32[]{:S(2)}, u32[]{:S(2)}) collective-permute-start(bf16[768,768]{1,0:T(8,128)(2,1)S(1)} %pad_maximum_fusion.refs_0_), channel_id=1, source_target_pairs={{0,8},{4,12},{8,0},{12,4},{16,24},{20,28},{24,16},{28,20},{1,9},{5... | collective-permute-start | bytes 3538952 | tf_op jit(solution)/shard_map/ppermute | solution.py:889
  268.5 24.9 %all-to-all-start.1 = ((bf16[4,2,288,128]{3,2,1,0:T(8,128)(2,1)}), bf16[4,2,288,128]{3,2,1,0:T(8,128)(2,1)S(1)}, u32[]{:S(2)}, u32[]{:S(2)}) async-start(bf16[4,2,288,128]{3,2,1,0:T(8,128)(2,1)} %broadcast_in_dim.16), calls=%async_computation.1 | async-start | bytes 1179648 | tf_op jit(solution)/shard_map/all_to_all | solution.py:893
  316.0 26.8 %collective-permute-start.32 = (bf16[512,768]{1,0:T(8,128)(2,1)}, bf16[512,768]{1,0:T(8,128)(2,1)}, u32[]{:S(2)}, u32[]{:S(2)}) collective-permute-start(bf16[512,768]{1,0:T(8,128)(2,1)} %add_convert_fusion.2), channel_id=1, source_target_pairs={{8,0},{12,4},{16,8},{20,12},{24,16},{28,20},{9,1},{13,5},{17,9},{2... | collective-permute-start | bytes 2359304 | tf_op jit(solution)/shard_map/ppermute | solution.py:899
  (77 other events, 814.4 us)

commit v3 on v1

--- a/solution.py
+++ b/solution.py
@@ -238,7 +238,7 @@
                 heads_ref[2 * g + h, here, :] = part
         return unused
 
-    lax.fori_loop(0, q_ref.shape[0] // TILE, some, 0)
+    lax.fori_loop(0, q_ref.shape[0] // TILE, some, 0, unroll=2)
 
 
 def tile_mask(begin, low, high):
@@ -390,7 +390,7 @@
                 grads_ref[2 * g + h, here, :] = part
         return unused
 
-    lax.fori_loop(0, total // TILE, begin, 0, unroll=2)
+    lax.fori_loop(0, total // TILE, begin, 0, unroll=4)
     waits[4]()
     put_heads(heads_ref, q_ref)
     waits[5]()
@@ -453,7 +453,7 @@
         return unused
 
     lax.fori_loop(0, total // TILE, finish_queries, 0)
-    lax.fori_loop(0, 2 * total // TILE, finish_keys, 0)
+    lax.fori_loop(0, 2 * total // TILE, finish_keys, 0, unroll=2)
 
 
 def attend_back(meta, q, k, v, own, sib, w_out, tall, logs, low):

time: 348 us -> 346 us (level)
  Pallas kernels: 184 us -> 179 us
    pallas_call x20, Pallas kernels: 184 us -> 179 us  [call(): pl.pallas_call(body, name=name, out_shape=out_shape, grid_spec=pltpu.Pref...]
  transfers between devices with their start and end apart: 52 -> 52, of which waited for: 16 -> 15; matrix products, arithmetic and copies ran while one was open for 6% -> 6% of each run, Pallas kernels for 50% -> 49%
where the time goes in v3:
time: 346 us; the launch traced here: 344 us
  Pallas kernels  179 us (52%)
  starting transfers between devices  70.9 us (20%)
  waiting for transfers between devices  58 us (17%)
  other arithmetic  20.1 us (6%)
  local copies, waits for them, and re-layouts  14.9 us (4%)
    pallas_call x20, Pallas kernels, call(): pl.pallas_call(body, name=name, out_shape=out_shape, grid_spec=pltpu.Pref...  179 us
    ppermute x48, waiting for transfers between devices, swap(): lax.ppermute(block, axis, [(i, i ^ distance) for i in range(lax.axis_size...  57.1 us
    ppermute x48, starting transfers between devices, swap(): lax.ppermute(block, axis, [(i, i ^ distance) for i in range(lax.axis_size...  56.4 us
    convert_element_type x10, other arithmetic, total(): return sum((t.astype(F32) for t in terms)).astype(BF16)  12.7 us
    unnamed x92, local copies, waits for them, and re-layouts  10.7 us
    all_to_all x2, starting transfers between devices, trade(): return lax.all_to_all(block, axis, split_axis=0, concat_axis=0, tiled=True)  8.73 us
  transfers between devices with their start and end apart: 52, of which 15 were waited for; matrix products, arithmetic and copies ran while one was open for 6% of the time, Pallas kernels for 49%

profile of v3, /device:TPU:0, one launch (start us, length us, event | category | flops | bytes accessed | tf_op | source)
XLA Modules:
  0.0 344.2 jit_solution(933777873869888844)
XLA Ops:
  7.6 5.0 %route.1 = (s32[512,1]{1,0:T(8,128)}, s32[1,1024]{1,0:T(1,128)}, s32[1024,1]{1,0:T(8,128)}, s32[1,128]{1,0:T(1,128)}, bf16[256,768]{1,0:T(8,128)(2,1)}, /*index=...) custom-call(s32[3]{0:T(128)} %pad_add_fusion.at_ref, s32[1,512]{1,0:T(1,128)} %ids_ref.1, ...), custom_call_target="tpu_custom_call" | custom-call | flops 1 | bytes 1 | tf_op jit(solution)/shard_map/route/pallas_call | solution.py:74
  14.8 7.6 %project.2 = (bf16[2048,768]{1,0:T(8,128)(2,1)}, bf16[2048,384]{1,0:T(8,128)(2,1)}, bf16[2048,384]{1,0:T(8,128)(2,1)}, bf16[1024,384]{1,0:T(8,128)(2,1)}) custom-call(s32[1]{0:T(128)} %bitcast.core_ref, bf16[512,768]{1,0:T(8,128)(2,1)} %bitcast.48, bf16[512,768]{1,0:T(8,128)(2,1)} %copy-done.6, f32[24,128]{1,0:T(8,128)} %pad_maximum_fusion.5.norm_ref, ...), custom_call_target="tpu_custom_call" | custom-call | flops 1 | bytes 1 | tf_op jit(solution)/shard_map/project/pallas_call | solution.py:74
  28.6 6.5 %project.3 = (bf16[2048,768]{1,0:T(8,128)(2,1)}, bf16[2048,384]{1,0:T(8,128)(2,1)}, bf16[2048,384]{1,0:T(8,128)(2,1)}) custom-call(s32[1]{0:T(128)} %bitcast.core_ref, bf16[512,768]{1,0:T(8,128)(2,1)} %copy-done.4, bf16[512,768]{1,0:T(8,128)(2,1)} %copy-done.5, ...), custom_call_target="tpu_custom_call", output_to_operand_aliasing={{0}: (7, {}), {1}: (8, {}), {2}: (9, {})} | custom-call | flops 1 | bytes 1 | tf_op jit(solution)/shard_map/project/pallas_call | solution.py:74
  35.1 16.8 %attend.1 = (bf16[512,384]{1,0:T(8,128)(2,1)}, bf16[512,384]{1,0:T(8,128)(2,1)}, bf16[1024,384]{1,0:T(8,128)(2,1)}, f32[384,1024]{1,0:T(8,128)}, f32[8,1024]{1,0:T(8,128)}) custom-call(s32[1,128]{1,0:T(1,128)} %get-tuple-element.174.meta_ref, bf16[1024,384]{1,0:T(8,128)(2,1)} %get-tuple-element.168.q_ref.q_hbm, ...), custom_call_target="tpu_custom_call" | custom-call | flops 1 | bytes 1 | tf_op jit(solution)/shard_map/attend/pallas_call | solution.py:74
  55.5 5.8 %lift.1 = (f32[512,768]{1,0:T(8,128)}, bf16[256,768]{1,0:T(8,128)(2,1)}, bf16[256,768]{1,0:T(8,128)(2,1)}, bf16[256,768]{1,0:T(8,128)(2,1)}, bf16[256,768]{1,0:T(8,128)(2,1)}) custom-call(s32[1]{0:T(128)} %bitcast.core_ref, bf16[512,384]{1,0:T(8,128)(2,1)} %get-tuple-element.178.own_ref, bf16[512,384]{1,0:T(8,128)(2,1)} %copy-done.35, ...), custom_call_target="tpu_custom_call" | custom-call | flops 1 | bytes 1 | tf_op jit(solution)/shard_map/lift/pallas_call | solution.py:74
  61.3 8.3 %collective-permute-start.7 = (bf16[256,768]{1,0:T(8,128)(2,1)}, bf16[256,768]{1,0:T(8,128)(2,1)S(1)}, u32[]{:S(2)}, u32[]{:S(2)}) collective-permute-start(bf16[256,768]{1,0:T(8,128)(2,1)} %get-tuple-element.188), channel_id=1, source_target_pairs={{0,1},{1,0},{2,3},{3,2},{4,5},{5,4},{6,7},{7,6},{8,9},{9,8},{10,11... | collective-permute-start | bytes 1179656 | tf_op jit(solution)/shard_map/ppermute | solution.py:889
  72.0 10.1 %expert.4 = (bf16[3072,256]{1,0:T(8,128)(2,1)}, bf16[256,3072]{1,0:T(8,128)(2,1)}, bf16[256,768]{1,0:T(8,128)(2,1)}, bf16[256,768]{1,0:T(8,128)(2,1)}, bf16[768,256]{1,0:T(8,128)(2,1)}) custom-call(bf16[256,768]{1,0:T(8,128)(2,1)} %get-tuple-element.186.rows_ref, bf16[256,768]{1,0:T(8,128)(2,1)} %get-tuple-element.180.grad_ref.refs_4_, ...), custom_call_target="tpu_custom_call" | custom-call | flops 1 | bytes 1 | tf_op jit(solution)/shard_map/expert/pallas_call | solution.py:74
  86.6 10.1 %expert.5 = (bf16[3072,256]{1,0:T(8,128)(2,1)}, bf16[256,3072]{1,0:T(8,128)(2,1)}, bf16[256,768]{1,0:T(8,128)(2,1)}, bf16[256,768]{1,0:T(8,128)(2,1)}, bf16[768,256]{1,0:T(8,128)(2,1)}) custom-call(bf16[256,768]{1,0:T(8,128)(2,1)} %copy-done.30, bf16[256,768]{1,0:T(8,128)(2,1)} %copy-done.16, bf16[768,3072]{1,0:T(8,128)(2,1)} %bitcast.39, ...), custom_call_target="tpu_custom_call" | custom-call | flops 1 | bytes 1 | tf_op jit(solution)/shard_map/expert/pallas_call | solution.py:74
  100.3 10.1 %expert.6 = (bf16[3072,256]{1,0:T(8,128)(2,1)}, bf16[256,3072]{1,0:T(8,128)(2,1)}, bf16[256,768]{1,0:T(8,128)(2,1)}, bf16[256,768]{1,0:T(8,128)(2,1)}, bf16[768,256]{1,0:T(8,128)(2,1)}) custom-call(bf16[256,768]{1,0:T(8,128)(2,1)} %copy-done.29, bf16[256,768]{1,0:T(8,128)(2,1)} %copy-done.17, bf16[768,3072]{1,0:T(8,128)(2,1)} %bitcast.40, ...), custom_call_target="tpu_custom_call" | custom-call | flops 1 | bytes 1 | tf_op jit(solution)/shard_map/expert/pallas_call | solution.py:74
  111.3 10.2 %expert.7 = (bf16[3072,256]{1,0:T(8,128)(2,1)}, bf16[256,3072]{1,0:T(8,128)(2,1)}, bf16[256,768]{1,0:T(8,128)(2,1)}, bf16[256,768]{1,0:T(8,128)(2,1)}, bf16[768,256]{1,0:T(8,128)(2,1)}) custom-call(bf16[256,768]{1,0:T(8,128)(2,1)} %copy-done.28, bf16[256,768]{1,0:T(8,128)(2,1)} %copy-done.18, bf16[768,3072]{1,0:T(8,128)(2,1)} %bitcast.41, ...), custom_call_target="tpu_custom_call" | custom-call | flops 1 | bytes 1 | tf_op jit(solution)/shard_map/expert/pallas_call | solution.py:74
  124.6 16.3 %expert_grad.1 = (bf16[1536,768]{1,0:T(8,128)(2,1)}, bf16[1536,768]{1,0:T(8,128)(2,1)}, bf16[1536,768]{1,0:T(8,128)(2,1)}, bf16[1536,768]{1,0:T(8,128)(2,1)}) custom-call(s32[5]{0:T(128)} %stack.52.chip_ref.meta_ref, bf16[768,256]{1,0:T(8,128)(2,1)} %get-tuple-element.202.refs_0_, bf16[768,256]{1,0:T(8,128)(2,1)} %get-tuple-element.203.refs_1_, ...), custom_call_target="tpu_custom_call" | custom-call | flops 1 | bytes 1 | tf_op jit(solution)/shard_map/expert_grad/pallas_call | solution.py:74
  141.8 5.3 %lower.1 = (f32[512,768]{1,0:T(8,128)}, bf16[512,768]{1,0:T(8,128)(2,1)}, f32[1,768]{1,0:T(1,128)}, f32[1,768]{1,0:T(1,128)}) custom-call(s32[512,1]{1,0:T(8,128)} %get-tuple-element.166.slot_ref, f32[512,768]{1,0:T(8,128)} %get-tuple-element.185.resid_ref, bf16[512,768]{1,0:T(8,128)(2,1)} %bitcast.57, f32[24,128]{1,0:T(8,128)} %pad_maximum_fusion.5.norm_ref, ...), custom_call_target="tpu_custom_call" | custom-call | flops 1 | bytes 1 | tf_op jit(solution)/shard_map/lower/pallas_call | solution.py:74
  164.2 18.2 %attend_back.1 = (bf16[1024,384]{1,0:T(8,128)(2,1)}, bf16[2048,384]{1,0:T(8,128)(2,1)}, bf16[2048,384]{1,0:T(8,128)(2,1)}) custom-call(s32[1,128]{1,0:T(1,128)} %get-tuple-element.174.meta_ref, bf16[1024,384]{1,0:T(8,128)(2,1)} %get-tuple-element.168.q_ref.q_hbm, bf16[2048,384]{1,0:T(8,128)(2,1)} %get-tuple-element.175.k_ref.k_hbm, ...), custom_call_target="tpu_custom_call" | custom-call | flops 1 | bytes 1 | tf_op jit(solution)/shard_map/attend_back/pallas_call | solution.py:74
  182.4 10.1 %dense.1 = (bf16[2304,128]{1,0:T(8,128)(2,1)}, bf16[2304,128]{1,0:T(8,128)(2,1)}, bf16[2304,128]{1,0:T(8,128)(2,1)}, bf16[2304,128]{1,0:T(8,128)(2,1)}) custom-call(s32[5]{0:T(128)} %stack.52.chip_ref.meta_ref, bf16[2048,768]{1,0:T(8,128)(2,1)} %get-tuple-element.173.a_hbm, bf16[1024,384]{1,0:T(8,128)(2,1)} %get-tuple-element.255.gq_hbm.gq_ref, ...), custom_call_target="tpu_custom_call" | custom-call | flops 1 | bytes 1 | tf_op jit(solution)/shard_map/dense/pallas_call | solution.py:74
  193.3 7.4 %collective-permute-start.19 = (bf16[2304,128]{1,0:T(8,128)(2,1)}, bf16[2304,128]{1,0:T(8,128)(2,1)S(1)}, u32[]{:S(2)}, u32[]{:S(2)}) collective-permute-start(bf16[2304,128]{1,0:T(8,128)(2,1)} %get-tuple-element.249), channel_id=1, source_target_pairs={{0,8},{4,12},{8,0},{12,4},{16,24},{20,28},{24,16},{28,20},{1,9},{5... | collective-permute-start | bytes 1769480 | tf_op jit(solution)/shard_map/ppermute | solution.py:889
  206.4 13.1 %project_back.1 = (f32[512,768]{1,0:T(8,128)}, bf16[1024,768]{1,0:T(8,128)(2,1)}, f32[512,768]{1,0:T(8,128)}, f32[1,768]{1,0:T(1,128)}, f32[1,768]{1,0:T(1,128)}) custom-call(s32[1]{0:T(128)} %bitcast.core_ref, bf16[512,768]{1,0:T(8,128)(2,1)} %bitcast.50, bf16[512,768]{1,0:T(8,128)(2,1)} %copy-done.6, bf16[512,768]{1,0:T(8,128)(2,1)} %copy-done.4, ...), custom_call_target="tpu_custom_call" | custom-call | flops 1 | bytes 1 | tf_op jit(solution)/shard_map/project_back/pallas_call | solution.py:74
  219.5 6.5 %collective-permute-done.24 = bf16[384,768]{1,0:T(8,128)(2,1)S(1)} collective-permute-done((bf16[384,768]{1,0:T(8,128)(2,1)}, bf16[384,768]{1,0:T(8,128)(2,1)S(1)}, u32[]{:S(2)}, u32[]{:S(2)}) %collective-permute-start.24) | collective-permute-done | bytes 589856 | tf_op jit(solution)/shard_map/ppermute | solution.py:889
  232.0 5.5 %collective-permute-done.26 = bf16[1152,128]{1,0:T(8,128)(2,1)S(1)} collective-permute-done((bf16[1152,128]{1,0:T(8,128)(2,1)S(1)}, bf16[1152,128]{1,0:T(8,128)(2,1)S(1)}, u32[]{:S(2)}, u32[]{:S(2)}) %collective-permute-start.26) | collective-permute-done | bytes 294944 | tf_op jit(solution)/shard_map/ppermute | solution.py:889
  252.7 6.5 %collective-permute-done.28 = bf16[384,768]{1,0:T(8,128)(2,1)} collective-permute-done((bf16[384,768]{1,0:T(8,128)(2,1)S(1)}, bf16[384,768]{1,0:T(8,128)(2,1)}, u32[]{:S(2)}, u32[]{:S(2)}) %collective-permute-start.28) | collective-permute-done | bytes 589856 | tf_op jit(solution)/shard_map/ppermute | solution.py:889
  265.4 4.8 %all-to-all-start.1 = ((bf16[4,2,288,128]{3,2,1,0:T(8,128)(2,1)}), bf16[4,2,288,128]{3,2,1,0:T(8,128)(2,1)S(1)}, u32[]{:S(2)}, u32[]{:S(2)}) async-start(bf16[4,2,288,128]{3,2,1,0:T(8,128)(2,1)} %broadcast_in_dim.16), calls=%async_computation.1 | async-start | bytes 1179648 | tf_op jit(solution)/shard_map/all_to_all | solution.py:893
  272.8 18.9 %collective-permute-done.36 = f32[4,768]{1,0:T(4,128)S(1)} collective-permute-done((f32[4,768]{1,0:T(4,128)S(1)}, f32[4,768]{1,0:T(4,128)S(1)}, u32[]{:S(2)}, u32[]{:S(2)}) %collective-permute-start.36) | collective-permute-done | bytes 12320 | tf_op jit(solution)/shard_map/ppermute | solution.py:889
  296.4 7.5 %widen.2 = (f32[768,3072]{1,0:T(8,128)}, f32[3072,768]{1,0:T(8,128)}) custom-call(s32[5]{0:T(128)} %stack.52.chip_ref.meta_ref, bf16[768,768]{1,0:T(8,128)(2,1)} %copy-done.2, bf16[768,768]{1,0:T(8,128)(2,1)} %collective-permute-done.32.refs_1_, bf16[768,768]{1,0:T(8,128)(2,1)} %copy-done.1, bf16[768,768]{1,0:T(8,128)(2,1)} %collective-permute-done.33.refs_3_), custom_call_target="tpu_custom_call" | custom-call | flops 1 | bytes 1 | tf_op jit(solution)/shard_map/widen/pallas_call | solution.py:74
  313.0 7.6 %widen.3 = (f32[768,3072]{1,0:T(8,128)}, f32[3072,768]{1,0:T(8,128)}) custom-call(s32[5]{0:T(128)} %stack.58.meta_ref, bf16[768,768]{1,0:T(8,128)(2,1)} %collective-permute-done.34.refs_0_, bf16[768,768]{1,0:T(8,128)(2,1)} %copy-done.20, bf16[768,768]{1,0:T(8,128)(2,1)} %collective-permute-done.35.refs_2_, ...), custom_call_target="tpu_custom_call", output_to_operand_aliasing={{0}: (5, {}), {1}: (6, {})} | custom-call | flops 1 | bytes 1 | tf_op jit(solution)/shard_map/widen/pallas_call | solution.py:74
  332.7 6.8 %spread_columns.1 = f32[768,2304]{1,0:T(8,128)} custom-call(s32[5]{0:T(128)} %stack.52.chip_ref.meta_ref, bf16[2,3,384,128]{3,2,1,0:T(8,128)(2,1)} %bitcast.64, bf16[2,3,384,128]{3,2,1,0:T(8,128)(2,1)} %bitcast.25.refs_1_, bf16[2,3,384,128]{3,2,1,0:T(8,128)(2,1)} %bitcast.55, bf16[2,3,384,128]{3,2,1,0:T(8,128)(2,1)} %bitcast.59, ...), custom_call_target="tpu_custom_call" | custom-call | flops 1 | bytes 1 | tf_op jit(solution)/shard_map/spread_columns/pallas_call | solution.py:74
  (222 shorter events, 118.0 us)
Async XLA Ops:
  1.2 22.2 %collective-permute-start = (bf16[512,768]{1,0:T(8,128)(2,1)}, bf16[512,768]{1,0:T(8,128)(2,1)S(1)}, u32[]{:S(2)}, u32[]{:S(2)}) collective-permute-start(bf16[512,768]{1,0:T(8,128)(2,1)} %bitcast.47), channel_id=1, source_target_pairs={{0,8},{4,12},{8,16},{12,20},{16,24},{20,28},{1,9},{5,13},{9,17},{1... | collective-permute-start | bytes 2359304 | tf_op jit(solution)/shard_map/ppermute | solution.py:899
  23.3 28.6 %collective-permute-start.4 = (bf16[256,768]{1,0:T(8,128)(2,1)S(1)}, bf16[256,768]{1,0:T(8,128)(2,1)S(1)}, u32[]{:S(2)}, u32[]{:S(2)}) collective-permute-start(bf16[256,768]{1,0:T(8,128)(2,1)S(1)} %copy-done.45), channel_id=1, source_target_pairs={{0,1},{1,0},{2,3},{3,2},{4,5},{5,4},{6,7},{7,6},{8,9},{9,8},{10,11... | collective-permute-start | bytes 1179656 | tf_op jit(solution)/shard_map/ppermute | solution.py:889
  24.9 29.7 %collective-permute-start.5 = (bf16[256,768]{1,0:T(8,128)(2,1)S(1)}, bf16[256,768]{1,0:T(8,128)(2,1)S(1)}, u32[]{:S(2)}, u32[]{:S(2)}) collective-permute-start(bf16[256,768]{1,0:T(8,128)(2,1)S(1)} %copy-done.44), channel_id=1, source_target_pairs={{0,2},{1,3},{2,0},{3,1},{4,6},{5,7},{6,4},{7,5},{8,10},{9,11},{10,... | collective-permute-start | bytes 1179656 | tf_op jit(solution)/shard_map/ppermute | solution.py:889
  27.5 27.2 %collective-permute-start.6 = (bf16[256,768]{1,0:T(8,128)(2,1)S(1)}, bf16[256,768]{1,0:T(8,128)(2,1)S(1)}, u32[]{:S(2)}, u32[]{:S(2)}) collective-permute-start(bf16[256,768]{1,0:T(8,128)(2,1)S(1)} %copy-done.43), channel_id=1, source_target_pairs={{0,3},{1,2},{2,1},{3,0},{4,7},{5,6},{6,5},{7,4},{8,11},{9,10},{10,... | collective-permute-start | bytes 1179656 | tf_op jit(solution)/shard_map/ppermute | solution.py:889
  61.3 24.6 %collective-permute-start.7 = (bf16[256,768]{1,0:T(8,128)(2,1)}, bf16[256,768]{1,0:T(8,128)(2,1)S(1)}, u32[]{:S(2)}, u32[]{:S(2)}) collective-permute-start(bf16[256,768]{1,0:T(8,128)(2,1)} %get-tuple-element.188), channel_id=1, source_target_pairs={{0,1},{1,0},{2,3},{3,2},{4,5},{5,4},{6,7},{7,6},{8,9},{9,8},{10,11... | collective-permute-start | bytes 1179656 | tf_op jit(solution)/shard_map/ppermute | solution.py:889
  69.5 30.0 %collective-permute-start.8 = (bf16[256,768]{1,0:T(8,128)(2,1)}, bf16[256,768]{1,0:T(8,128)(2,1)S(1)}, u32[]{:S(2)}, u32[]{:S(2)}) collective-permute-start(bf16[256,768]{1,0:T(8,128)(2,1)} %get-tuple-element.192), channel_id=1, source_target_pairs={{0,2},{1,3},{2,0},{3,1},{4,6},{5,7},{6,4},{7,5},{8,10},{9,11},{10,... | collective-permute-start | bytes 1179656 | tf_op jit(solution)/shard_map/ppermute | solution.py:889
  70.6 40.0 %collective-permute-start.9 = (bf16[256,768]{1,0:T(8,128)(2,1)}, bf16[256,768]{1,0:T(8,128)(2,1)S(1)}, u32[]{:S(2)}, u32[]{:S(2)}) collective-permute-start(bf16[256,768]{1,0:T(8,128)(2,1)} %get-tuple-element.196), channel_id=1, source_target_pairs={{0,3},{1,2},{2,1},{3,0},{4,7},{5,6},{6,5},{7,4},{8,11},{9,10},{10,... | collective-permute-start | bytes 1179656 | tf_op jit(solution)/shard_map/ppermute | solution.py:889
  96.7 27.9 %collective-permute-start.10 = (bf16[256,768]{1,0:T(8,128)(2,1)}, bf16[256,768]{1,0:T(8,128)(2,1)S(1)}, u32[]{:S(2)}, u32[]{:S(2)}) collective-permute-start(bf16[256,768]{1,0:T(8,128)(2,1)} %get-tuple-element.193), channel_id=1, source_target_pairs={{0,1},{1,0},{2,3},{3,2},{4,5},{5,4},{6,7},{7,6},{8,9},{9,8},{10,11... | collective-permute-start | bytes 1179656 | tf_op jit(solution)/shard_map/ppermute | solution.py:889
  110.4 30.5 %collective-permute-start.11 = (bf16[256,768]{1,0:T(8,128)(2,1)}, bf16[256,768]{1,0:T(8,128)(2,1)S(1)}, u32[]{:S(2)}, u32[]{:S(2)}) collective-permute-start(bf16[256,768]{1,0:T(8,128)(2,1)} %get-tuple-element.197), channel_id=1, source_target_pairs={{0,2},{1,3},{2,0},{3,1},{4,6},{5,7},{6,4},{7,5},{8,10},{9,11},{10,... | collective-permute-start | bytes 1179656 | tf_op jit(solution)/shard_map/ppermute | solution.py:889
  153.3 47.4 %collective-permute-start.22 = (bf16[768,768]{1,0:T(8,128)(2,1)}, bf16[768,768]{1,0:T(8,128)(2,1)}, u32[]{:S(2)}, u32[]{:S(2)}) collective-permute-start(bf16[768,768]{1,0:T(8,128)(2,1)} %add_convert_fusion), channel_id=1, source_target_pairs={{0,16},{4,20},{8,24},{12,28},{16,0},{20,4},{24,8},{28,12},{1,17},{... | collective-permute-start | bytes 3538952 | tf_op jit(solution)/shard_map/ppermute | solution.py:889
  157.9 42.8 %collective-permute-start.21 = (bf16[768,768]{1,0:T(8,128)(2,1)}, bf16[768,768]{1,0:T(8,128)(2,1)}, u32[]{:S(2)}, u32[]{:S(2)}) collective-permute-start(bf16[768,768]{1,0:T(8,128)(2,1)} %add_convert_fusion.1), channel_id=1, source_target_pairs={{0,8},{4,12},{8,0},{12,4},{16,24},{20,28},{24,16},{28,20},{1,9},{5... | collective-permute-start | bytes 3538952 | tf_op jit(solution)/shard_map/ppermute | solution.py:889
  158.5 33.9 %collective-permute-start.16 = (bf16[256,768]{1,0:T(8,128)(2,1)}, bf16[256,768]{1,0:T(8,128)(2,1)S(1)}, u32[]{:S(2)}, u32[]{:S(2)}) collective-permute-start(bf16[256,768]{1,0:T(8,128)(2,1)} %get-tuple-element.245), channel_id=1, source_target_pairs={{0,1},{1,0},{2,3},{3,2},{4,5},{5,4},{6,7},{7,6},{8,9},{9,8},{10,11... | collective-permute-start | bytes 1179656 | tf_op jit(solution)/shard_map/ppermute | solution.py:889
  161.8 30.7 %collective-permute-start.17 = (bf16[256,768]{1,0:T(8,128)(2,1)}, bf16[256,768]{1,0:T(8,128)(2,1)}, u32[]{:S(2)}, u32[]{:S(2)}) collective-permute-start(bf16[256,768]{1,0:T(8,128)(2,1)} %get-tuple-element.246), channel_id=1, source_target_pairs={{0,2},{1,3},{2,0},{3,1},{4,6},{5,7},{6,4},{7,5},{8,10},{9,11},{10,... | collective-permute-start | bytes 1179656 | tf_op jit(solution)/shard_map/ppermute | solution.py:889
  162.3 30.2 %collective-permute-start.18 = (bf16[256,768]{1,0:T(8,128)(2,1)}, bf16[256,768]{1,0:T(8,128)(2,1)}, u32[]{:S(2)}, u32[]{:S(2)}) collective-permute-start(bf16[256,768]{1,0:T(8,128)(2,1)} %get-tuple-element.247), channel_id=1, source_target_pairs={{0,3},{1,2},{2,1},{3,0},{4,7},{5,6},{6,5},{7,4},{8,11},{9,10},{10,... | collective-permute-start | bytes 1179656 | tf_op jit(solution)/shard_map/ppermute | solution.py:889
  193.3 26.2 %collective-permute-start.19 = (bf16[2304,128]{1,0:T(8,128)(2,1)}, bf16[2304,128]{1,0:T(8,128)(2,1)S(1)}, u32[]{:S(2)}, u32[]{:S(2)}) collective-permute-start(bf16[2304,128]{1,0:T(8,128)(2,1)} %get-tuple-element.249), channel_id=1, source_target_pairs={{0,8},{4,12},{8,0},{12,4},{16,24},{20,28},{24,16},{28,20},{1,9},{5... | collective-permute-start | bytes 1769480 | tf_op jit(solution)/shard_map/ppermute | solution.py:889
  203.0 23.1 %collective-permute-start.24 = (bf16[384,768]{1,0:T(8,128)(2,1)}, bf16[384,768]{1,0:T(8,128)(2,1)S(1)}, u32[]{:S(2)}, u32[]{:S(2)}) collective-permute-start(bf16[384,768]{1,0:T(8,128)(2,1)} %add_convert_fusion.7), channel_id=1, source_target_pairs={{0,8},{4,12},{8,0},{12,4},{16,24},{20,28},{24,16},{28,20},{1,9},{5... | collective-permute-start | bytes 1769480 | tf_op jit(solution)/shard_map/ppermute | solution.py:889
  204.3 23.2 %collective-permute-start.23 = (bf16[384,768]{1,0:T(8,128)(2,1)S(1)}, bf16[384,768]{1,0:T(8,128)(2,1)S(1)}, u32[]{:S(2)}, u32[]{:S(2)}) collective-permute-start(bf16[384,768]{1,0:T(8,128)(2,1)S(1)} %add_convert_fusion.8), channel_id=1, source_target_pairs={{0,16},{4,20},{8,24},{12,28},{16,0},{20,4},{24,8},{28,12},{1,17},{... | collective-permute-start | bytes 1769480 | tf_op jit(solution)/shard_map/ppermute | solution.py:889
  230.5 22.2 %collective-permute-start.29 = (bf16[384,768]{1,0:T(8,128)(2,1)S(1)}, bf16[384,768]{1,0:T(8,128)(2,1)}, u32[]{:S(2)}, u32[]{:S(2)}) collective-permute-start(bf16[384,768]{1,0:T(8,128)(2,1)S(1)} %add_convert_fusion.3), channel_id=1, source_target_pairs={{0,8},{4,12},{8,0},{12,4},{16,24},{20,28},{24,16},{28,20},{1,9},{5... | collective-permute-start | bytes 1769480 | tf_op jit(solution)/shard_map/ppermute | solution.py:889
  262.9 28.8 %collective-permute-start.34 = (bf16[768,768]{1,0:T(8,128)(2,1)S(1)}, bf16[768,768]{1,0:T(8,128)(2,1)}, u32[]{:S(2)}, u32[]{:S(2)}) collective-permute-start(bf16[768,768]{1,0:T(8,128)(2,1)S(1)} %pad_maximum_fusion.refs_0_), channel_id=1, source_target_pairs={{0,4},{4,0},{8,12},{12,8},{16,20},{20,16},{24,28},{28,24},{1,5},{5... | collective-permute-start | bytes 3538952 | tf_op jit(solution)/shard_map/ppermute | solution.py:889
  263.0 28.7 %collective-permute-start.35 = (bf16[768,768]{1,0:T(8,128)(2,1)S(1)}, bf16[768,768]{1,0:T(8,128)(2,1)}, u32[]{:S(2)}, u32[]{:S(2)}) collective-permute-start(bf16[768,768]{1,0:T(8,128)(2,1)S(1)} %pad_maximum_fusion.1.refs_2_), channel_id=1, source_target_pairs={{0,4},{4,0},{8,12},{12,8},{16,20},{20,16},{24,28},{28,24},{1,5},{5... | collective-permute-start | bytes 3538952 | tf_op jit(solution)/shard_map/ppermute | solution.py:889
  263.5 28.2 %collective-permute-start.33 = (bf16[768,768]{1,0:T(8,128)(2,1)S(1)}, bf16[768,768]{1,0:T(8,128)(2,1)}, u32[]{:S(2)}, u32[]{:S(2)}) collective-permute-start(bf16[768,768]{1,0:T(8,128)(2,1)S(1)} %pad_maximum_fusion.1.refs_2_), channel_id=1, source_target_pairs={{0,16},{4,20},{8,24},{12,28},{16,0},{20,4},{24,8},{28,12},{1,17},{... | collective-permute-start | bytes 3538952 | tf_op jit(solution)/shard_map/ppermute | solution.py:889
  263.7 28.0 %collective-permute-start.32 = (bf16[768,768]{1,0:T(8,128)(2,1)S(1)}, bf16[768,768]{1,0:T(8,128)(2,1)}, u32[]{:S(2)}, u32[]{:S(2)}) collective-permute-start(bf16[768,768]{1,0:T(8,128)(2,1)S(1)} %pad_maximum_fusion.refs_0_), channel_id=1, source_target_pairs={{0,8},{4,12},{8,0},{12,4},{16,24},{20,28},{24,16},{28,20},{1,9},{5... | collective-permute-start | bytes 3538952 | tf_op jit(solution)/shard_map/ppermute | solution.py:889
  265.4 26.2 %all-to-all-start.1 = ((bf16[4,2,288,128]{3,2,1,0:T(8,128)(2,1)}), bf16[4,2,288,128]{3,2,1,0:T(8,128)(2,1)S(1)}, u32[]{:S(2)}, u32[]{:S(2)}) async-start(bf16[4,2,288,128]{3,2,1,0:T(8,128)(2,1)} %broadcast_in_dim.16), calls=%async_computation.1 | async-start | bytes 1179648 | tf_op jit(solution)/shard_map/all_to_all | solution.py:893
  311.1 29.0 %collective-permute-start.31 = (bf16[512,768]{1,0:T(8,128)(2,1)}, bf16[512,768]{1,0:T(8,128)(2,1)}, u32[]{:S(2)}, u32[]{:S(2)}) collective-permute-start(bf16[512,768]{1,0:T(8,128)(2,1)} %add_convert_fusion.2), channel_id=1, source_target_pairs={{8,0},{12,4},{16,8},{20,12},{24,16},{28,20},{9,1},{13,5},{17,9},{2... | collective-permute-start | bytes 2359304 | tf_op jit(solution)/shard_map/ppermute | solution.py:899
  (74 other events, 737.9 us)
